TPU v7x, 512 devices: a whole 4x8x8 slice. The times are simulated.
512 devices in a mesh: lon: 32 (over z_lo, y), lat: 8 (over x, core), section: 2 (over z_hi).
Axes of the slice: x: 4, y: 8, z: 8 (z_hi: 2, z_lo: 4; z = z_hi * 4 + z_lo), core: 2. Of those that a mesh axis runs over, the one named last changes fastest.
Arguments:
- upper_fields: bfloat16 [5, 6, 192, 1536], P(None, None, 'lat', 'lon'), may hold values from -6 to 6
- surface_fields: bfloat16 [4, 192, 1536], P(None, 'lat', 'lon'), may hold values from -6 to 6
- upper_embed: bfloat16 [160, 192], replicated, may hold values from -0.5 to 0.5
- surface_embed: bfloat16 [64, 192], replicated, may hold values from -0.75 to 0.75
- norm_gains: float32 [2, 2, 192], replicated, may hold values from 0.1 to 1.9
- qkv_weight: bfloat16 [2, 192, 576], replicated, may hold values from -0.4375 to 0.4375
- proj_weight: bfloat16 [2, 192, 192], replicated, may hold values from -0.4375 to 0.4375
- up_weight: bfloat16 [2, 192, 768], replicated, may hold values from -0.4375 to 0.4375
- down_weight: bfloat16 [2, 768, 192], replicated, may hold values from -0.21875 to 0.21875
- earth_bias: float32 [2, 8, 2, 6, 3312], P(None, 'lat', 'section'), may hold values from -4 to 402
- out_grad: bfloat16 [4, 48, 384, 192], P('section', 'lat', 'lon'), may hold values from -6 to 6
Outputs:
- latent_grad: bfloat16 [4, 48, 384, 192], P('section', 'lat', 'lon')
- upper_embed_grad: float32 [160, 192], replicated
- surface_embed_grad: float32 [64, 192], replicated
All inputs are finite; a program needn't handle non-finite values.
Results may differ from a plain program's by a relative error of at most 0.024.
Values may be sent and summed in bfloat16 or wider, within the bound.
A program may use at most 64 MiB of HBM per device.

v0:
```python
import jax
import jax.numpy as jnp
import numpy as np
from jax import lax
from jax.sharding import PartitionSpec as P

neg_fill = -1e30
norm_eps = 1e-05


def shifted(block, axis, distance):
    devices = range(lax.axis_size(axis))
    route = [((i - distance) % len(devices), i) for i in devices]
    return lax.ppermute(block, axis, route)


def layer_norm(values, gain):
    average = jnp.mean(values, -1, keepdims=True)
    centred = values - average
    variance = jnp.mean(centred * centred, -1, keepdims=True)
    return centred * lax.rsqrt(variance + norm_eps) * gain


def exact_gelu(values):
    return jax.nn.gelu(values, approximate=False)


def pinned_round(values):
    return lax.optimization_barrier(values.astype(jnp.bfloat16)).astype(jnp.float32)


def make_patches(upper_fields, surface_fields):
    up_vars, raw_levels, raw_rows, raw_cols = upper_fields.shape
    upper_patch = upper_fields.reshape(
        up_vars, raw_levels // 2, 2, raw_rows // 4, 4, raw_cols // 4, 4
    )
    upper_patch = upper_patch.transpose(1, 3, 5, 0, 2, 4, 6).reshape(
        raw_levels // 2, raw_rows // 4, raw_cols // 4, up_vars * 32
    )
    sf_vars = surface_fields.shape[0]
    surface_patch = surface_fields.reshape(sf_vars, raw_rows // 4, 4, raw_cols // 4, 4)
    surface_patch = surface_patch.transpose(1, 3, 0, 2, 4).reshape(
        raw_rows // 4, raw_cols // 4, sf_vars * 16
    )
    return (upper_patch, surface_patch)


def to_windows(volume):
    levels, rows, cols, channels = volume.shape
    split = volume.reshape(levels // 2, 2, rows // 6, 6, cols // 12, 12, channels)
    return split.transpose(0, 2, 4, 1, 3, 5, 6).reshape(
        levels // 2, rows // 6, cols // 12, 144, channels
    )


def from_windows(windows):
    zone_z, zone_lat, zone_lon, cells, channels = windows.shape
    split = windows.reshape(zone_z, zone_lat, zone_lon, 2, 6, 12, channels)
    return split.transpose(0, 3, 1, 4, 2, 5, 6).reshape(
        zone_z * 2, zone_lat * 6, zone_lon * 12, channels
    )


def bias_index():
    token = np.arange(144)
    level_part = token // 72
    row_part = token // 12 % 6
    col_part = token % 12
    pair = (
        (level_part[:, None] * 2 + level_part[None, :]) * 36
        + row_part[:, None] * 6
        + row_part[None, :]
    )
    return pair * 23 + col_part[:, None] - col_part[None, :] + 11


def window_bias(table):
    return table[..., bias_index()]


def region_valid(level_base, row_base, levels_total, rows_total, zone_z, zone_lat):
    level = level_base + jnp.arange(zone_z * 2, dtype=jnp.int32)
    row = row_base + jnp.arange(zone_lat * 6, dtype=jnp.int32)
    zone_level = (level >= levels_total - 2).astype(jnp.int32) + (level >= levels_total - 1).astype(
        jnp.int32
    )
    zone_row = (row >= rows_total - 6).astype(jnp.int32) + (row >= rows_total - 3).astype(jnp.int32)
    labels = zone_level.reshape(zone_z, 1, 2, 1, 1) * 3 + zone_row.reshape(1, zone_lat, 1, 6, 1)
    labels = (labels + jnp.zeros((1, 1, 1, 1, 12), jnp.int32)).reshape(zone_z, zone_lat, 144)
    return labels[:, :, :, None] == labels[:, :, None, :]


def attention_forward(qkv_win, bias, allowed):
    zone_z, zone_lat, zone_lon, cells, channels = qkv_win.shape
    head_count = bias.shape[2]
    head_size = channels // (3 * head_count)
    parts = qkv_win.reshape(zone_z, zone_lat, zone_lon, cells, 3, head_count, head_size)
    query = parts[:, :, :, :, 0]
    keys_all = parts[:, :, :, :, 1]
    values_all = parts[:, :, :, :, 2]
    score = jnp.einsum("zlwqhd,zlwkhd->zlwhqk", query, keys_all, preferred_element_type=jnp.float32)
    score = score * head_size ** (-0.5) + bias[:, :, None]
    score = jnp.where(allowed[:, :, None, None], score, neg_fill)
    highest = jnp.max(score, -1, keepdims=True)
    expo = jnp.exp(score - highest)
    prob = expo / jnp.sum(expo, -1, keepdims=True)
    weights = prob.astype(jnp.bfloat16)
    mixed = jnp.einsum(
        "zlwhqk,zlwkhd->zlwqhd", weights, values_all, preferred_element_type=jnp.float32
    )
    mixed = mixed.astype(jnp.bfloat16).reshape(zone_z, zone_lat, zone_lon, cells, channels // 3)
    return (mixed, (query, keys_all, values_all, prob, weights))


def attention_backward(dmixed_win, saved):
    query, keys_all, values_all, prob, weights = saved
    head_size = query.shape[-1]
    dmixed = dmixed_win.reshape(query.shape)
    dweights = jnp.einsum(
        "zlwqhd,zlwkhd->zlwhqk", dmixed, values_all, preferred_element_type=jnp.float32
    )
    dweights = pinned_round(dweights)
    dvalues = jnp.einsum(
        "zlwhqk,zlwqhd->zlwkhd", weights, dmixed, preferred_element_type=jnp.float32
    )
    inner = jnp.sum(dweights * prob, -1, keepdims=True)
    dscore = prob * (dweights - inner) * head_size ** (-0.5)
    dquery = jnp.einsum(
        "zlwhqk,zlwkhd->zlwqhd",
        dscore,
        keys_all.astype(jnp.float32),
        precision=lax.Precision.HIGHEST,
    )
    dkeys = jnp.einsum(
        "zlwhqk,zlwqhd->zlwkhd", dscore, query.astype(jnp.float32), precision=lax.Precision.HIGHEST
    )
    stacked = jnp.stack((dquery, dkeys, dvalues), 4).astype(jnp.bfloat16)
    shape = stacked.shape
    return stacked.reshape(shape[0], shape[1], shape[2], shape[3], shape[4] * shape[5] * shape[6])


def block_forward(volume, params, bias, allowed, final):
    gains, w_qkv, w_proj, w_up, w_down = params
    levels, rows, cols, width = volume.shape
    inputs = volume.reshape(-1, width).astype(jnp.float32)
    hidden = layer_norm(inputs, gains[0]).astype(jnp.bfloat16)
    qkv_rows = jnp.dot(hidden, w_qkv, preferred_element_type=jnp.float32).astype(jnp.bfloat16)
    qkv_win = to_windows(qkv_rows.reshape(levels, rows, cols, 3 * width))
    mixed_win, attend_saved = attention_forward(qkv_win, bias, allowed)
    mixed = from_windows(mixed_win).reshape(-1, width)
    resid = inputs + jnp.dot(mixed, w_proj, preferred_element_type=jnp.float32)
    normed = layer_norm(resid, gains[1]).astype(jnp.bfloat16)
    upward = jnp.dot(normed, w_up, preferred_element_type=jnp.float32)
    active = exact_gelu(upward).astype(jnp.bfloat16)
    saved = (volume.shape, inputs, attend_saved, resid, upward)
    if final:
        return (None, saved)
    output = resid + jnp.dot(active, w_down, preferred_element_type=jnp.float32)
    return (output.astype(jnp.bfloat16).reshape(volume.shape), saved)


def block_backward(dvolume, saved, params):
    gains, w_qkv, w_proj, w_up, w_down = params
    shape, inputs, attend_saved, resid, upward = saved
    levels, rows, cols, width = shape
    dflat = dvolume.reshape(-1, width)
    dactive = pinned_round(jnp.dot(dflat, w_down.T, preferred_element_type=jnp.float32))
    dupward = jax.vjp(exact_gelu, upward)[1](dactive)[0]
    dnormed = jnp.dot(dupward, w_up.astype(jnp.float32).T, precision=lax.Precision.HIGHEST)
    dnormed = pinned_round(dnormed)
    dresid = dflat.astype(jnp.float32) + jax.vjp(layer_norm, resid, gains[1])[1](dnormed)[0]
    dmixed = jnp.dot(dresid, w_proj.astype(jnp.float32).T, precision=lax.Precision.HIGHEST).astype(
        jnp.bfloat16
    )
    dqkv_win = attention_backward(
        to_windows(dmixed.reshape(levels, rows, cols, width)), attend_saved
    )
    dqkv = from_windows(dqkv_win).reshape(-1, 3 * width)
    dhidden = pinned_round(jnp.dot(dqkv, w_qkv.T, preferred_element_type=jnp.float32))
    dinputs = dresid + jax.vjp(layer_norm, inputs, gains[0])[1](dhidden)[0]
    return dinputs.astype(jnp.bfloat16).reshape(shape)


def move_edge(volume, axis_dim, edge_depth, direction, sender):
    length = volume.shape[axis_dim]
    if direction > 0:
        border = lax.slice_in_dim(volume, 0, edge_depth, axis=axis_dim)
        remain = lax.slice_in_dim(volume, edge_depth, length, axis=axis_dim)
        return jnp.concatenate((remain, sender(border)), axis_dim)
    border = lax.slice_in_dim(volume, length - edge_depth, length, axis=axis_dim)
    remain = lax.slice_in_dim(volume, 0, length - edge_depth, axis=axis_dim)
    return jnp.concatenate((sender(border), remain), axis_dim)


def roll_rows_levels(volume, direction):
    volume = move_edge(volume, 1, 3, direction, lambda border: shifted(border, "lat", -direction))
    return move_edge(volume, 0, 1, direction, lambda border: shifted(border, "section", -direction))


def roll_columns(volume, direction):
    return move_edge(volume, 2, 6, direction, lambda border: shifted(border, "lon", -direction))


def to_shifted(volume):
    volume = roll_rows_levels(volume, 1)
    return roll_columns(volume, 1)


def on_device(
    upper_fields,
    surface_fields,
    upper_embed,
    surface_embed,
    norm_gains,
    qkv_weight,
    proj_weight,
    up_weight,
    down_weight,
    earth_bias,
    out_grad,
):
    section_index = lax.axis_index("section")
    band_index = lax.axis_index("lat")
    level_count, row_count, column_count, width = out_grad.shape
    levels_total = level_count * lax.axis_size("section")
    rows_total = row_count * lax.axis_size("lat")
    upper_patch, surface_patch = make_patches(upper_fields, surface_fields)
    upper_latent = jnp.einsum(
        "zyxp,pc->zyxc", upper_patch, upper_embed, preferred_element_type=jnp.float32
    )
    surface_latent = jnp.einsum(
        "yxp,pc->yxc", surface_patch, surface_embed, preferred_element_type=jnp.float32
    )
    latent_all = jnp.concatenate((surface_latent[None], upper_latent), 0).astype(jnp.bfloat16)
    latent = lax.dynamic_slice_in_dim(latent_all, section_index * level_count, level_count, 0)
    zone_z = level_count // 2
    zone_lat = row_count // 6
    params_first = (norm_gains[0], qkv_weight[0], proj_weight[0], up_weight[0], down_weight[0])
    params_second = (norm_gains[1], qkv_weight[1], proj_weight[1], up_weight[1], down_weight[1])
    bias_first = window_bias(earth_bias[0].transpose(1, 0, 2, 3))
    bias_second = window_bias(earth_bias[1].transpose(1, 0, 2, 3))
    allow_all = jnp.ones((zone_z, zone_lat, 144, 144), jnp.bool_)
    allow_shifted = region_valid(
        section_index * level_count,
        band_index * row_count,
        levels_total,
        rows_total,
        zone_z,
        zone_lat,
    )
    first_out, first_saved = block_forward(latent, params_first, bias_first, allow_all, False)
    unused_out, second_saved = block_forward(
        to_shifted(first_out), params_second, bias_second, allow_shifted, True
    )
    dshifted = block_backward(to_shifted(out_grad), second_saved, params_second)
    dshifted = roll_columns(dshifted, -1)
    dmiddle = roll_rows_levels(dshifted, -1)
    latent_grad = block_backward(dmiddle, first_saved, params_first)
    spread_grad = jnp.zeros((levels_total, row_count, column_count, width), jnp.bfloat16)
    spread_grad = lax.dynamic_update_slice_in_dim(
        spread_grad, latent_grad, section_index * level_count, 0
    )
    upper_terms = jnp.einsum(
        "zyxp,zyxc->pc", upper_patch, spread_grad[1:], preferred_element_type=jnp.float32
    )
    surface_terms = jnp.einsum(
        "yxp,yxc->pc", surface_patch, spread_grad[0], preferred_element_type=jnp.float32
    )
    upper_total, surface_total = lax.psum((upper_terms, surface_terms), ("lon", "lat", "section"))
    scale = float(levels_total * rows_total * column_count * lax.axis_size("lon")) ** (-0.5)
    return (latent_grad, upper_total * scale, surface_total * scale)


def solution(mesh):
    placed = (
        P(None, None, "lat", "lon"),
        P(None, "lat", "lon"),
        P(),
        P(),
        P(),
        P(),
        P(),
        P(),
        P(),
        P(None, "lat", "section", None, None),
        P("section", "lat", "lon", None),
    )
    return jax.shard_map(
        on_device,
        mesh=mesh,
        in_specs=placed,
        out_specs=(P("section", "lat", "lon", None), P(), P()),
        check_vma=False,
    )
```

profile of v0, /device:TPU:1, one launch (start us, length us, event | category | flops | bytes accessed | tf_op | source)
XLA Modules:
  0.0 605.3 jit_solution(6361948579435595958)
XLA Ops:
  7.2 3.6 reshape.639
  10.9 5.5 copy.49
  16.3 1.1 reshape.637
  18.1 1.5 convolution_convert_fusion.6
  19.6 1.0 fusion.18
  21.6 1.4 fusion.265
  23.1 1.2 convolution_convert_fusion.5
  25.7 0.9 pad_clamp_fusion
  26.6 38.7 %gather_fusion = f32[20736,6]{1,0:T(8,128)} fusion(f32[6,3312]{0,1:T(8,128)S(1)} %bitcast.205, s32[21504]{0:T(1024)S(1)} %pad_clamp_fusion), kind=kCustom, calls=%fused_computation | custom fusion | bytes 1078272 | tf_op jit(solution)/shard_map/gather | solution.py:78
  65.3 11.7 %copy.54 = f32[144,144,6]{0,1,2:T(8,128)S(1)} copy(f32[144,144,6]{2,1,0:T(8,128)} %bitcast.208) | data formatting | bytes 995328 | tf_op jit(solution)/shard_map/gather | solution.py:78
  77.3 1.1 fusion.268
  79.3 2.1 fusion.48
  83.1 6.9 %collective-permute-start.3 = (bf16[2,3,12,192]{3,2,1,0:T(8,128)(2,1)}, bf16[2,3,12,192]{3,2,1,0:T(8,128)(2,1)}, u32[]{:S(2)}, u32[]{:S(2)}) collective-permute-start(bf16[2,3,12,192]{3,2,1,0:T(8,128)(2,1)} %get-tuple-element.28), channel_id=1, source_target_pairs={{2,0},{4,2},{6,4},{8,6},{10,8},{12,10},{14,12},{0,14},{3,1},{5,3},... | collective-permute-start | bytes 82952 | tf_op jit(solution)/shard_map/ppermute | solution.py:14
  91.7 1.4 copy.97
  93.1 38.7 %gather_fusion.1 = f32[20736,6]{1,0:T(8,128)} fusion(f32[6,3312]{0,1:T(8,128)S(1)} %bitcast.206, s32[21504]{0:T(1024)S(1)} %pad_clamp_fusion), kind=kCustom, calls=%fused_computation.1 | custom fusion | bytes 1078272 | tf_op jit(solution)/shard_map/gather | solution.py:78
  131.8 11.7 %copy.59 = f32[144,144,6]{0,1,2:T(8,128)S(1)} copy(f32[144,144,6]{2,1,0:T(8,128)} %bitcast.207) | data formatting | bytes 995328 | tf_op jit(solution)/shard_map/gather | solution.py:78
  143.5 0.8 fusion.205
  144.3 7.4 %collective-permute-start.4 = (bf16[1,6,12,192]{3,2,1,0:T(8,128)(2,1)S(1)}, bf16[1,6,12,192]{3,2,1,0:T(8,128)(2,1)S(1)}, u32[]{:S(2)}, u32[]{:S(2)}) collective-permute-start(bf16[1,6,12,192]{3,2,1,0:T(8,128)(2,1)S(1)} %get-tuple-element.26), channel_id=1, source_target_pairs={{1,0},{0,1},{3,2},{2,3},{5,4},{4,5},{7,6},{6,7},{9,8},{8,9},{11,10... | collective-permute-start | bytes 82952 | tf_op jit(solution)/shard_map/ppermute | solution.py:14
  151.8 1.0 slice_maximum_fusion
  152.8 1.9 collective-permute-start.1
  154.8 7.8 %collective-permute-start.5 = (bf16[2,6,6,192]{3,2,1,0:T(8,128)(2,1)S(1)}, bf16[2,6,6,192]{3,2,1,0:T(8,128)(2,1)S(1)}, u32[]{:S(2)}, u32[]{:S(2)}) collective-permute-start(bf16[2,6,6,192]{3,2,1,0:T(8,128)(2,1)S(1)} %get-tuple-element.24), channel_id=1, source_target_pairs={{16,0},{32,16},{48,32},{64,48},{80,64},{96,80},{112,96},{128,112},... | collective-permute-start | bytes 82952 | tf_op jit(solution)/shard_map/ppermute | solution.py:14
  162.6 0.8 fusion.206
  163.4 7.4 %collective-permute-start.2 = (bf16[2,6,6,192]{3,0,2,1:T(2,128)(2,1)}, bf16[2,6,6,192]{3,0,2,1:T(2,128)(2,1)}, u32[]{:S(2)}, u32[]{:S(2)}) collective-permute-start(bf16[2,6,6,192]{3,0,2,1:T(2,128)(2,1)} %get-tuple-element.18), channel_id=1, source_target_pairs={{16,0},{32,16},{48,32},{64,48},{80,64},{96,80},{112,96},{128,112},... | collective-permute-start | bytes 82952 | tf_op jit(solution)/shard_map/ppermute | solution.py:14
  171.9 0.9 convolution_convert_fusion.4
  172.8 1.8 copy.56
  174.6 2.2 fusion.7
  176.8 2.6 fusion.270
  179.4 1.8 convolution_convert_fusion.13
  181.3 1.2 fusion.271
  182.7 0.9 pad_maximum_fusion.6
  183.9 1.2 fusion.123
  185.2 2.4 convolution_convert_fusion.18
  187.6 0.9 multiply_reduce_fusion.5
  188.5 0.9 fusion.258
  190.5 1.2 fusion.9
  191.7 1.4 fusion.19
  193.1 2.4 fusion.12
  195.5 2.5 fusion.13
  198.0 1.8 fusion.16
  199.9 1.0 pad_maximum_fusion
  202.4 0.8 add_convert_fusion.1
  203.4 2.1 collective-permute-start.6
  205.4 6.8 %collective-permute-done.6 = bf16[2,6,6,192]{3,2,1,0:T(8,128)(2,1)S(1)} collective-permute-done((bf16[2,6,6,192]{3,2,1,0:T(8,128)(2,1)S(1)}, bf16[2,6,6,192]{3,2,1,0:T(8,128)(2,1)S(1)}, u32[]{:S(2)}, u32[]{:S(2)}) %collective-permute-start.6) | collective-permute-done | bytes 27680 | tf_op jit(solution)/shard_map/ppermute | solution.py:14
  212.3 2.2 collective-permute-start.7
  214.5 1.9 collective-permute-done.7
  216.4 2.6 collective-permute-start.8
  219.7 1.3 add.178
  221.0 4.1 collective-permute-done.8
  225.2 1.2 convolution_convert_fusion.2
  226.4 1.8 convolution_convert_fusion.16
  228.2 0.9 multiply_reduce_fusion.3
  229.8 0.9 fusion.257
  230.7 1.2 convolution_convert_fusion.19
  232.0 1.2 fusion.10
  233.4 1.4 fusion.14
  234.8 2.2 fusion.15
  237.4 1.0 pad_maximum_fusion.1
  238.7 0.8 multiply_reduce_fusion.2
  239.5 0.9 fusion.256
  240.4 0.8 add_convert_fusion
  241.5 2.1 convolution_bitcast_fusion
  243.6 96.8 %psum.15 = f32[64,192]{1,0:T(8,128)S(1)} all-reduce(f32[64,192]{1,0:T(8,128)S(1)} %convolution_bitcast_fusion.1), channel_id=1, replica_groups=mesh['lon'=32,'lat'=8,'section'=2] {'lon','lat','section'}, use_global_device_ids=true, to_apply=%region_23.24 | all-reduce | flops 12288 | bytes 98304 | tf_op jit(solution)/shard_map/psum | solution.py:269
  341.7 255.1 %all-reduce.2.cloned.1.call-done = f32[160,192]{1,0:T(8,128)} async-done(((f32[160,192]{1,0:T(8,128)}), f32[160,192]{1,0:T(8,128)}) %all-reduce.2.cloned.1.call-update) | async-done | bytes 122896 | tf_op jit(solution)/shard_map/psum | solution.py:269
  596.8 1.6 broadcast_multiply_fusion
  (136 shorter events, 16.2 us)
Async XLA Ops:
  7.2 11.0 %copy-start = (bf16[160,192]{1,0:T(8,128)(2,1)S(1)}, bf16[160,192]{1,0:T(8,128)(2,1)}, u32[]{:S(2)}) copy-start(bf16[160,192]{1,0:T(8,128)(2,1)} %param.17) | copy-start | bytes 184324
  7.2 17.2 %copy-start.14 = (f32[2,1,1,6,3312]{4,2,3,1,0:T(1,128)S(1)}, f32[2,1,1,6,3312]{4,2,3,1,0:T(1,128)}, u32[]{:S(2)}) copy-start(f32[2,1,1,6,3312]{4,2,3,1,0:T(1,128)} %param.24) | copy-start | bytes 476932
  7.2 589.6 %all-reduce.2.cloned.1.call-start = ((), (), s32[]{:S(2)}) async-start(), calls=%async_computation | async-start | bytes 327680 | tf_op jit(solution)/shard_map/psum | solution.py:269
  18.1 7.0 %copy-start.6 = (bf16[6,12,4,4,4]{1,4,3,2,0:T(4,128)(2,1)}, bf16[6,12,4,4,4]{1,4,3,2,0:T(4,128)(2,1)S(1)}, u32[]{:S(2)}) copy-start(bf16[6,12,4,4,4]{1,4,3,2,0:T(4,128)(2,1)S(1)} %copy.47) | copy-start | bytes 27652
  22.9 3.7 copy-start.18
  24.4 54.0 %copy-start.5 = (bf16[144,576]{0,1:T(8,128)(2,1)}, bf16[144,576]{0,1:T(8,128)(2,1)S(1)}, u32[]{:S(2)}) copy-start(bf16[144,576]{0,1:T(8,128)(2,1)S(1)} %copy.51) | copy-start | bytes 497668
  65.3 13.5 %copy-start.8 = (bf16[2,192,192]{2,1,0:T(8,128)(2,1)S(1)}, bf16[2,192,192]{2,1,0:T(8,128)(2,1)}, u32[]{:S(2)}) copy-start(bf16[2,192,192]{2,1,0:T(8,128)(2,1)} %param.21) | copy-start | bytes 442372
  65.3 14.1 %copy-start.22 = (f32[1,1,192]{2,1,0:T(1,128)S(1)}, f32[1,1,192]{2,1,0:T(1,128)}, u32[]{:S(2)}) copy-start(f32[1,1,192]{2,1,0:T(1,128)} %get-tuple-element.38) | copy-start | bytes 2308
  77.0 5.2 copy-start.3
  77.0 13.1 %copy-start.16 = (bf16[2,6,12,192]{3,0,2,1:T(2,128)(2,1)S(1)}, bf16[2,6,12,192]{3,0,2,1:T(2,128)(2,1)}, u32[]{:S(2)}) copy-start(bf16[2,6,12,192]{3,0,2,1:T(2,128)(2,1)} %param.25) | copy-start | bytes 165892
  79.1 12.6 %copy-start.20 = (f32[144]{0:T(256)}, f32[144]{0:T(256)S(1)}, u32[]{:S(2)}) copy-start(f32[144]{0:T(256)S(1)} %broadcast_multiply_fusion.5) | copy-start | bytes 1732
  79.3 12.4 %copy-start.23 = (f32[144]{0:T(256)}, f32[144]{0:T(256)S(1)}, u32[]{:S(2)}) copy-start(f32[144]{0:T(256)S(1)} %multiply_reduce_fusion.7) | copy-start | bytes 1732
  79.3 12.4 %copy-start.24 = (f32[144]{0:T(256)}, f32[144]{0:T(256)S(1)}, u32[]{:S(2)}) copy-start(f32[144]{0:T(256)S(1)} %fusion.208) | copy-start | bytes 1732
  81.4 0.8 copy-start.11
  81.4 10.3 %copy-start.10 = (f32[144,768]{1,0:T(8,128)}, f32[144,768]{1,0:T(8,128)S(1)}, u32[]{:S(2)}) copy-start(f32[144,768]{1,0:T(8,128)S(1)} %get-tuple-element.49) | copy-start | bytes 1327108
  83.1 60.4 %collective-permute-start.3 = (bf16[2,3,12,192]{3,2,1,0:T(8,128)(2,1)}, bf16[2,3,12,192]{3,2,1,0:T(8,128)(2,1)}, u32[]{:S(2)}, u32[]{:S(2)}) collective-permute-start(bf16[2,3,12,192]{3,2,1,0:T(8,128)(2,1)} %get-tuple-element.28), channel_id=1, source_target_pairs={{2,0},{4,2},{6,4},{8,6},{10,8},{12,10},{14,12},{0,14},{3,1},{5,3},... | collective-permute-start | bytes 82952 | tf_op jit(solution)/shard_map/ppermute | solution.py:14
  90.7 61.1 %collective-permute-start = (bf16[2,3,12,192]{3,0,2,1:T(2,128)(2,1)}, bf16[2,3,12,192]{3,0,2,1:T(2,128)(2,1)}, u32[]{:S(2)}, u32[]{:S(2)}) collective-permute-start(bf16[2,3,12,192]{3,0,2,1:T(2,128)(2,1)} %get-tuple-element.32), channel_id=1, source_target_pairs={{2,0},{4,2},{6,4},{8,6},{10,8},{12,10},{14,12},{0,14},{3,1},{5,3},... | collective-permute-start | bytes 82952 | tf_op jit(solution)/shard_map/ppermute | solution.py:14
  93.1 78.8 %copy-start.2 = (bf16[2,192,576]{2,1,0:T(8,128)(2,1)S(1)}, bf16[2,192,576]{2,1,0:T(8,128)(2,1)}, u32[]{:S(2)}) copy-start(bf16[2,192,576]{2,1,0:T(8,128)(2,1)} %param.20) | copy-start | bytes 1327108
  131.8 11.7 %copy-start.13 = (bf16[2,3,12,192]{3,2,1,0:T(8,128)(2,1)S(1)}, bf16[2,3,12,192]{3,2,1,0:T(8,128)(2,1)}, u32[]{:S(2)}) copy-start(bf16[2,3,12,192]{3,2,1,0:T(8,128)(2,1)} %get-tuple-element.27) | copy-start | bytes 82948
  131.8 20.0 %copy-start.15 = (bf16[2,3,12,192]{3,0,2,1:T(2,128)(2,1)S(1)}, bf16[2,3,12,192]{3,0,2,1:T(2,128)(2,1)}, u32[]{:S(2)}) copy-start(bf16[2,3,12,192]{3,0,2,1:T(2,128)(2,1)} %get-tuple-element.31) | copy-start | bytes 82948
  131.8 51.9 %copy-start.4 = (bf16[2,768,192]{1,2,0:T(8,128)(2,1)S(1)}, bf16[2,768,192]{1,2,0:T(8,128)(2,1)}, u32[]{:S(2)}) copy-start(bf16[2,768,192]{1,2,0:T(8,128)(2,1)} %param.23) | copy-start | bytes 1769476
  144.3 10.4 %collective-permute-start.4 = (bf16[1,6,12,192]{3,2,1,0:T(8,128)(2,1)S(1)}, bf16[1,6,12,192]{3,2,1,0:T(8,128)(2,1)S(1)}, u32[]{:S(2)}, u32[]{:S(2)}) collective-permute-start(bf16[1,6,12,192]{3,2,1,0:T(8,128)(2,1)S(1)} %get-tuple-element.26), channel_id=1, source_target_pairs={{1,0},{0,1},{3,2},{2,3},{5,4},{4,5},{7,6},{6,7},{9,8},{8,9},{11,10... | collective-permute-start | bytes 82952 | tf_op jit(solution)/shard_map/ppermute | solution.py:14
  152.8 9.8 %collective-permute-start.1 = (bf16[1,6,12,192]{3,0,2,1:T(2,128)(2,1)S(1)}, bf16[1,6,12,192]{3,0,2,1:T(2,128)(2,1)S(1)}, u32[]{:S(2)}, u32[]{:S(2)}) collective-permute-start(bf16[1,6,12,192]{3,0,2,1:T(2,128)(2,1)S(1)} %get-tuple-element.30), channel_id=1, source_target_pairs={{1,0},{0,1},{3,2},{2,3},{5,4},{4,5},{7,6},{6,7},{9,8},{8,9},{11,10... | collective-permute-start | bytes 82952 | tf_op jit(solution)/shard_map/ppermute | solution.py:14
  154.8 16.0 %collective-permute-start.5 = (bf16[2,6,6,192]{3,2,1,0:T(8,128)(2,1)S(1)}, bf16[2,6,6,192]{3,2,1,0:T(8,128)(2,1)S(1)}, u32[]{:S(2)}, u32[]{:S(2)}) collective-permute-start(bf16[2,6,6,192]{3,2,1,0:T(8,128)(2,1)S(1)} %get-tuple-element.24), channel_id=1, source_target_pairs={{16,0},{32,16},{48,32},{64,48},{80,64},{96,80},{112,96},{128,112},... | collective-permute-start | bytes 82952 | tf_op jit(solution)/shard_map/ppermute | solution.py:14
  163.4 19.3 %collective-permute-start.2 = (bf16[2,6,6,192]{3,0,2,1:T(2,128)(2,1)}, bf16[2,6,6,192]{3,0,2,1:T(2,128)(2,1)}, u32[]{:S(2)}, u32[]{:S(2)}) collective-permute-start(bf16[2,6,6,192]{3,0,2,1:T(2,128)(2,1)} %get-tuple-element.18), channel_id=1, source_target_pairs={{16,0},{32,16},{48,32},{64,48},{80,64},{96,80},{112,96},{128,112},... | collective-permute-start | bytes 82952 | tf_op jit(solution)/shard_map/ppermute | solution.py:14
  176.8 12.6 %copy-start.9 = (bf16[2,192,192]{2,1,0:T(8,128)(2,1)S(1)}, bf16[2,192,192]{2,1,0:T(8,128)(2,1)}, u32[]{:S(2)}) copy-start(bf16[2,192,192]{2,1,0:T(8,128)(2,1)} %param.21) | copy-start | bytes 442372
  179.4 4.5 copy-start.17
  189.4 8.6 %copy-start.21 = (f32[144]{0:T(256)}, f32[144]{0:T(256)S(1)}, u32[]{:S(2)}) copy-start(f32[144]{0:T(256)S(1)} %negate_multiply_fusion.7) | copy-start | bytes 1732
  189.9 0.6 copy-start.12
  191.7 41.5 %copy-start.1 = (f32[6,144,144]{1,2,0:T(8,128)S(1)}, f32[6,144,144]{1,2,0:T(8,128)}, u32[]{:S(2)}) copy-start(f32[6,144,144]{1,2,0:T(8,128)} %get-tuple-element.46) | copy-start | bytes 1492996
  203.3 37.9 %copy-start.7 = (bf16[6,12,4,4,4]{1,4,3,2,0:T(4,128)(2,1)S(1)}, bf16[6,12,4,4,4]{1,4,3,2,0:T(4,128)(2,1)}, u32[]{:S(2)}) copy-start(bf16[6,12,4,4,4]{1,4,3,2,0:T(4,128)(2,1)} %copy-done.6) | copy-start | bytes 27652
  203.4 8.9 %collective-permute-start.6 = (bf16[2,6,6,192]{3,2,1,0:T(8,128)(2,1)S(1)}, bf16[2,6,6,192]{3,2,1,0:T(8,128)(2,1)S(1)}, u32[]{:S(2)}, u32[]{:S(2)}) collective-permute-start(bf16[2,6,6,192]{3,2,1,0:T(8,128)(2,1)S(1)} %get-tuple-element.21), channel_id=1, source_target_pairs={{496,0},{0,16},{16,32},{32,48},{48,64},{64,80},{80,96},{96,112},{1... | collective-permute-start | bytes 82952 | tf_op jit(solution)/shard_map/ppermute | solution.py:14
  212.3 4.1 collective-permute-start.7
  216.4 8.7 %collective-permute-start.8 = (bf16[1,6,12,192]{3,2,1,0:T(8,128)(2,1)S(1)}, bf16[1,6,12,192]{3,2,1,0:T(8,128)(2,1)S(1)}, u32[]{:S(2)}, u32[]{:S(2)}) collective-permute-start(bf16[1,6,12,192]{3,2,1,0:T(8,128)(2,1)S(1)} %get-tuple-element.19), channel_id=1, source_target_pairs={{1,0},{0,1},{3,2},{2,3},{5,4},{4,5},{7,6},{6,7},{9,8},{8,9},{11,10... | collective-permute-start | bytes 82952 | tf_op jit(solution)/shard_map/ppermute | solution.py:14
  225.1 13.5 %copy-start.19 = (f32[144]{0:T(256)S(1)}, f32[144]{0:T(256)}, u32[]{:S(2)}) copy-start(f32[144]{0:T(256)} %div.130) | copy-start | bytes 1732
  225.1 14.4 %copy-start.25 = (f32[144]{0:T(256)S(1)}, f32[144]{0:T(256)}, u32[]{:S(2)}) copy-start(f32[144]{0:T(256)} %add.178) | copy-start | bytes 1732
Sparse Core Ops, SparseCore 0:
  340.5 256.2 all-reduce.1
where the time goes:
time: 607 us; the launch traced here: 605 us
  waiting for transfers between devices  268 us (44%)
  local copies, waits for them, and re-layouts  125 us (21%)
  blocking collectives  96.8 us (16%)
  starting transfers between devices  38.4 us (6%)
  matrix products  37.3 us (6%)
  other arithmetic  25.4 us (4%)
  between operations  14.8 us (2%)
    psum x1, waiting for transfers between devices, on_device(): lax.psum((upper_terms, surface_terms), ('lon', 'lat', 'section'))  255 us
    gather x4, local copies, waits for them, and re-layouts, window_bias(): return table[..., bias_index()]  101 us
    psum x1, blocking collectives, on_device(): lax.psum((upper_terms, surface_terms), ('lon', 'lat', 'section'))  96.8 us
    ppermute x9, starting transfers between devices, shifted(): return lax.ppermute(block, axis, route)  38.4 us
    ppermute x9, waiting for transfers between devices, shifted(): return lax.ppermute(block, axis, route)  12.8 us
  transfers between devices with their start and end apart: 10, of which 4 were waited for; matrix products, arithmetic and copies ran while one was open for 12% of the time, Pallas kernels for 0%

commit v1 on v0

--- a/solution.py
+++ b/solution.py
@@ -2,6 +2,8 @@
 import jax.numpy as jnp
 import numpy as np
 from jax import lax
+from jax.experimental import pallas as pl
+from jax.experimental.pallas import tpu as pltpu
 from jax.sharding import PartitionSpec as P
 
 neg_fill = -1e30
@@ -266,9 +268,144 @@
     surface_terms = jnp.einsum(
         "yxp,yxc->pc", surface_patch, spread_grad[0], preferred_element_type=jnp.float32
     )
-    upper_total, surface_total = lax.psum((upper_terms, surface_terms), ("lon", "lat", "section"))
+    upper_total, surface_total = total_over_devices(upper_terms, surface_terms)
     scale = float(levels_total * rows_total * column_count * lax.axis_size("lon")) ** (-0.5)
     return (latent_grad, upper_total * scale, surface_total * scale)
+
+
+MESH = pl.DeviceIdType.MESH
+
+
+def wait_bytes(buffer, count, sem):
+    pltpu.make_async_copy(buffer.at[pl.ds(0, count)], buffer.at[pl.ds(0, count)], sem).wait()
+
+
+def total_kernel(terms, result, held, piece, across, last, sems):
+    lon_count = lax.axis_size("lon")
+    lat_count = lax.axis_size("lat")
+    section_count = lax.axis_size("section")
+    owners = terms.shape[0]
+    lon = lax.axis_index("lon")
+    lat = lax.axis_index("lat")
+    section = lax.axis_index("section")
+    group = lat_count * section_count
+    mine = section * lat_count + lat
+    barrier = pltpu.get_barrier_semaphore()
+
+    def greet_lon(d, carry):
+        pl.semaphore_signal(barrier, inc=1, device_id={"lon": lax.rem(lon + d, lon_count)}, device_id_type=MESH)
+        return carry
+
+    lax.fori_loop(1, lon_count, greet_lon, 0)
+
+    def peer_of(d):
+        other = lax.rem(mine + d, group)
+        return {"lat": lax.rem(other, lat_count), "section": other // lat_count}
+
+    def greet_group(d, carry):
+        pl.semaphore_signal(barrier, inc=1, device_id=peer_of(d), device_id_type=MESH)
+        return carry
+
+    lax.fori_loop(1, group, greet_group, 0)
+    pl.semaphore_wait(barrier, lon_count - 1 + group - 1)
+
+    def scatter(d, carry):
+        peer = lax.rem(lon + d, lon_count)
+
+        @pl.when(peer < owners)
+        def _():
+            pltpu.make_async_remote_copy(
+                src_ref=terms.at[peer],
+                dst_ref=held.at[d - 1],
+                send_sem=sems.at[0],
+                recv_sem=sems.at[1],
+                device_id={"lon": peer},
+                device_id_type=MESH,
+            ).start()
+
+        return carry
+
+    lax.fori_loop(1, lon_count, scatter, 0)
+
+    @pl.when(lon < owners)
+    def _():
+        wait_bytes(held, lon_count - 1, sems.at[1])
+        total = terms[lon].astype(jnp.float32)
+        for d in range(lon_count - 1):
+            total = total + held[d].astype(jnp.float32)
+        piece[...] = total.astype(piece.dtype)
+        across[mine] = total.astype(piece.dtype)
+
+        def exchange(d, carry):
+            pltpu.make_async_remote_copy(
+                src_ref=piece,
+                dst_ref=across.at[mine],
+                send_sem=sems.at[2],
+                recv_sem=sems.at[3],
+                device_id=peer_of(d),
+                device_id_type=MESH,
+            ).start()
+            return carry
+
+        lax.fori_loop(1, group, exchange, 0)
+        wait_bytes(across, group - 1, sems.at[3])
+        whole = across[0].astype(jnp.float32)
+        for d in range(1, group):
+            whole = whole + across[d].astype(jnp.float32)
+        last[...] = whole.astype(last.dtype)
+        result[lon] = whole.astype(last.dtype)
+
+        def gather(d, carry):
+            pltpu.make_async_remote_copy(
+                src_ref=last,
+                dst_ref=result.at[lon],
+                send_sem=sems.at[4],
+                recv_sem=sems.at[5],
+                device_id={"lon": lax.rem(lon + d, lon_count)},
+                device_id_type=MESH,
+            ).start()
+            return carry
+
+        lax.fori_loop(1, lon_count, gather, 0)
+        wait_bytes(terms, owners - 1, sems.at[0])
+        wait_bytes(across, group - 1, sems.at[2])
+        wait_bytes(result, owners - 1, sems.at[5])
+        wait_bytes(held, lon_count - 1, sems.at[4])
+
+    @pl.when(lon >= owners)
+    def _():
+        wait_bytes(terms, owners, sems.at[0])
+        wait_bytes(result, owners, sems.at[5])
+
+
+def total_over_devices(upper_terms, surface_terms):
+    terms = jnp.concatenate((upper_terms, surface_terms), 0).astype(jnp.bfloat16)
+    rows, width = terms.shape
+    low = terms[:, 128:]
+    packed = jnp.concatenate(
+        (terms[:, :128], jnp.concatenate((low[: rows // 2], low[rows // 2 :]), 1)), 0
+    ).reshape(-1, 16, 128)
+    lon_count = lax.axis_size("lon")
+    group = lax.axis_size("lat") * lax.axis_size("section")
+    total = pl.pallas_call(
+        total_kernel,
+        out_shape=jax.ShapeDtypeStruct(packed.shape, packed.dtype),
+        in_specs=[pl.BlockSpec(memory_space=pltpu.VMEM)],
+        out_specs=pl.BlockSpec(memory_space=pltpu.VMEM),
+        scratch_shapes=[
+            pltpu.VMEM((lon_count - 1, 16, 128), jnp.bfloat16),
+            pltpu.VMEM((16, 128), jnp.bfloat16),
+            pltpu.VMEM((group, 16, 128), jnp.bfloat16),
+            pltpu.VMEM((16, 128), jnp.bfloat16),
+            pltpu.SemaphoreType.DMA((6,)),
+        ],
+        compiler_params=pltpu.CompilerParams(collective_id=0, has_side_effects=True),
+    )(packed)
+    total = total.reshape(-1, 128).astype(jnp.float32)
+    low = total[rows:]
+    low = jnp.concatenate((low[:, :64], low[:, 64:]), 0)
+    whole = jnp.concatenate((total[:rows], low), 1)
+    return whole[: upper_terms.shape[0]], whole[upper_terms.shape[0] :]
 
 
 def solution(mesh):

time: 607 us -> 267 us (0.44)
  waiting for transfers between devices: 268 us -> 14.1 us
  blocking collectives: 96.8 us -> 0 us
  Pallas kernels: 0 us -> 28.6 us
  between operations: 14.8 us -> 1.64 us
    psum x1 -> x0, waiting for transfers between devices: 255 us -> none  [on_device(): lax.psum((upper_terms, surface_terms), ('lon', 'lat', 'section'))]
    psum x1 -> x0, blocking collectives: 96.8 us -> none  [on_device(): lax.psum((upper_terms, surface_terms), ('lon', 'lat', 'section'))]
    pallas_call x0 -> x1, Pallas kernels: none -> 28.6 us  [total_over_devices(): pl.pallas_call(total_kernel, out_shape=jax.ShapeDtypeStruct(packed.shape,...]
  transfers between devices with their start and end apart: 10 -> 9, of which waited for: 4 -> 3; matrix products, arithmetic and copies ran while one was open for 12% -> 23% of each run, Pallas kernels for 0% -> 0%
where the time goes in v1:
time: 267 us; the launch traced here: 265 us
  local copies, waits for them, and re-layouts  120 us (45%)
  starting transfers between devices  38.4 us (14%)
  matrix products  35.3 us (13%)
  Pallas kernels  28.6 us (11%)
  other arithmetic  27.1 us (10%)
  waiting for transfers between devices  14.1 us (5%)
    gather x4, local copies, waits for them, and re-layouts, window_bias(): return table[..., bias_index()]  101 us
    ppermute x9, starting transfers between devices, shifted(): return lax.ppermute(block, axis, route)  38.4 us
    pallas_call x1, Pallas kernels, total_over_devices(): pl.pallas_call(total_kernel, out_shape=jax.ShapeDtypeStruct(packed.shape,...  28.6 us
    ppermute x9, waiting for transfers between devices, shifted(): return lax.ppermute(block, axis, route)  14.1 us
    transpose x1, local copies, waits for them, and re-layouts, make_patches(): upper_patch.transpose(1, 3, 5, 0, 2, 4, 6)  5.46 us
  transfers between devices with their start and end apart: 9, of which 3 were waited for; matrix products, arithmetic and copies ran while one was open for 23% of the time, Pallas kernels for 0%

profile of v1, /device:TPU:1, one launch (start us, length us, event | category | flops | bytes accessed | tf_op | source)
XLA Modules:
  0.0 265.4 jit_solution(4006775552469966435)
XLA Ops:
  0.7 3.7 %reshape.645 = bf16[5,3,2,6,4,12,4]{6,5,4,3,2,1,0:T(8,128)(2,1)S(1)} reshape(bf16[5,6,24,48]{3,2,1,0:T(8,128)(2,1)} %param.15) | data formatting | bytes 138240 | tf_op jit(solution)/shard_map/reshape | solution.py:36
  4.3 5.5 %copy.49 = bf16[3,6,12,5,2,4,4]{2,6,5,4,3,1,0:T(4,128)(2,1)} copy(bf16[3,6,12,5,2,4,4]{6,2,5,1,4,0,3:T(8,128)(2,1)S(1)} %bitcast.220) | data formatting | bytes 138240 | tf_op jit(solution)/shard_map/transpose | solution.py:39
  9.8 1.1 reshape.643
  11.6 1.5 convolution_convert_fusion.6
  13.1 1.0 fusion.21
  15.0 1.4 fusion.279
  16.6 1.2 convolution_convert_fusion.5
  18.5 0.9 pad_clamp_fusion
  19.4 38.7 %gather_fusion = f32[20736,6]{1,0:T(8,128)} fusion(f32[6,3312]{0,1:T(8,128)S(1)} %bitcast.216, s32[21504]{0:T(1024)S(1)} %pad_clamp_fusion), kind=kCustom, calls=%fused_computation | custom fusion | bytes 1078272 | tf_op jit(solution)/shard_map/gather | solution.py:80
  58.1 11.7 %copy.54 = f32[144,144,6]{0,1,2:T(8,128)S(1)} copy(f32[144,144,6]{2,1,0:T(8,128)} %bitcast.219) | data formatting | bytes 995328 | tf_op jit(solution)/shard_map/gather | solution.py:80
  70.1 1.1 fusion.282
  72.1 2.1 fusion.52
  75.2 6.9 %collective-permute-start.3 = (bf16[2,3,12,192]{3,2,1,0:T(8,128)(2,1)}, bf16[2,3,12,192]{3,2,1,0:T(8,128)(2,1)}, u32[]{:S(2)}, u32[]{:S(2)}) collective-permute-start(bf16[2,3,12,192]{3,2,1,0:T(8,128)(2,1)} %get-tuple-element.30), channel_id=1, source_target_pairs={{2,0},{4,2},{6,4},{8,6},{10,8},{12,10},{14,12},{0,14},{3,1},{5,3},... | collective-permute-start | bytes 82952 | tf_op jit(solution)/shard_map/ppermute | solution.py:16
  84.3 38.7 %gather_fusion.1 = f32[20736,6]{1,0:T(8,128)} fusion(f32[6,3312]{0,1:T(8,128)S(1)} %bitcast.217, s32[21504]{0:T(1024)S(1)} %pad_clamp_fusion), kind=kCustom, calls=%fused_computation.1 | custom fusion | bytes 1078272 | tf_op jit(solution)/shard_map/gather | solution.py:80
  123.0 11.7 %copy.59 = f32[144,144,6]{0,1,2:T(8,128)S(1)} copy(f32[144,144,6]{2,1,0:T(8,128)} %bitcast.218) | data formatting | bytes 995328 | tf_op jit(solution)/shard_map/gather | solution.py:80
  134.7 0.8 fusion.218
  135.5 7.4 %collective-permute-start.4 = (bf16[1,6,12,192]{3,2,1,0:T(8,128)(2,1)S(1)}, bf16[1,6,12,192]{3,2,1,0:T(8,128)(2,1)S(1)}, u32[]{:S(2)}, u32[]{:S(2)}) collective-permute-start(bf16[1,6,12,192]{3,2,1,0:T(8,128)(2,1)S(1)} %get-tuple-element.28), channel_id=1, source_target_pairs={{1,0},{0,1},{3,2},{2,3},{5,4},{4,5},{7,6},{6,7},{9,8},{8,9},{11,10... | collective-permute-start | bytes 82952 | tf_op jit(solution)/shard_map/ppermute | solution.py:16
  142.9 1.0 slice_maximum_fusion
  143.9 1.9 collective-permute-start.1
  145.9 7.8 %collective-permute-start.5 = (bf16[2,6,6,192]{3,2,1,0:T(8,128)(2,1)S(1)}, bf16[2,6,6,192]{3,2,1,0:T(8,128)(2,1)S(1)}, u32[]{:S(2)}, u32[]{:S(2)}) collective-permute-start(bf16[2,6,6,192]{3,2,1,0:T(8,128)(2,1)S(1)} %get-tuple-element.26), channel_id=1, source_target_pairs={{16,0},{32,16},{48,32},{64,48},{80,64},{96,80},{112,96},{128,112},... | collective-permute-start | bytes 82952 | tf_op jit(solution)/shard_map/ppermute | solution.py:16
  153.8 0.8 fusion.219
  154.6 7.4 %collective-permute-start.2 = (bf16[2,6,6,192]{3,0,2,1:T(2,128)(2,1)}, bf16[2,6,6,192]{3,0,2,1:T(2,128)(2,1)}, u32[]{:S(2)}, u32[]{:S(2)}) collective-permute-start(bf16[2,6,6,192]{3,0,2,1:T(2,128)(2,1)} %get-tuple-element.20), channel_id=1, source_target_pairs={{16,0},{32,16},{48,32},{64,48},{80,64},{96,80},{112,96},{128,112},... | collective-permute-start | bytes 82952 | tf_op jit(solution)/shard_map/ppermute | solution.py:16
  164.5 1.1 fusion.284
  166.0 1.2 fusion.285
  167.4 0.9 pad_maximum_fusion.6
  168.4 1.2 convolution_convert_fusion.3
  169.6 1.2 fusion.127
  170.8 2.4 convolution_convert_fusion.18
  174.2 1.2 fusion.9
  175.4 1.4 fusion.23
  176.8 2.4 fusion.13
  179.2 2.6 fusion.14
  181.8 1.0 fusion.17
  182.9 1.1 pad_maximum_fusion
  183.9 1.3 convolution_convert_fusion.17
  185.3 0.8 multiply_reduce_fusion.4
  186.2 0.9 fusion.268
  187.0 1.1 add_convert_fusion.1
  188.2 2.1 collective-permute-start.6
  190.2 6.8 %collective-permute-done.6 = bf16[2,6,6,192]{3,2,1,0:T(8,128)(2,1)S(1)} collective-permute-done((bf16[2,6,6,192]{3,2,1,0:T(8,128)(2,1)S(1)}, bf16[2,6,6,192]{3,2,1,0:T(8,128)(2,1)S(1)}, u32[]{:S(2)}, u32[]{:S(2)}) %collective-permute-start.6) | collective-permute-done | bytes 27680 | tf_op jit(solution)/shard_map/ppermute | solution.py:16
  197.1 2.2 collective-permute-start.7
  199.3 1.9 collective-permute-done.7
  201.2 2.6 collective-permute-start.8
  204.6 5.4 %collective-permute-done.8 = bf16[1,6,12,192]{3,2,1,0:T(8,128)(2,1)S(1)} collective-permute-done((bf16[1,6,12,192]{3,2,1,0:T(8,128)(2,1)S(1)}, bf16[1,6,12,192]{3,2,1,0:T(8,128)(2,1)S(1)}, u32[]{:S(2)}, u32[]{:S(2)}) %collective-permute-start.8) | collective-permute-done | bytes 27680 | tf_op jit(solution)/shard_map/ppermute | solution.py:16
  210.6 0.8 pad_maximum_fusion.4
  211.5 1.2 convolution_convert_fusion.2
  212.7 1.8 convolution_convert_fusion.16
  214.5 0.9 multiply_reduce_fusion.3
  216.0 0.9 fusion.270
  217.0 1.3 convolution_convert_fusion.19
  218.3 0.7 copy.66
  219.0 1.3 fusion.10
  220.3 0.9 fusion.27
  221.1 2.1 fusion.15
  223.2 2.2 fusion.16
  225.5 1.2 fusion.18
  226.7 1.0 pad_maximum_fusion.1
  228.0 0.9 multiply_reduce_fusion.2
  228.9 0.9 fusion.269
  229.8 0.8 add_convert_fusion
  231.1 1.1 fusion.22
  232.9 28.6 %shard_map.166 = bf16[21,16,128]{2,1,0:T(8,128)(2,1)} custom-call(bf16[21,16,128]{2,1,0:T(8,128)(2,1)} %bitcast.245), custom_call_target="tpu_custom_call" | custom-call | tf_op jit(solution)/shard_map/pallas_call | solution.py:390
  261.6 0.9 convert_element_type.298
  262.5 0.8 slice.247
  (158 shorter events, 16.8 us)
Async XLA Ops:
  0.6 11.0 %copy-start = (bf16[160,192]{1,0:T(8,128)(2,1)S(1)}, bf16[160,192]{1,0:T(8,128)(2,1)}, u32[]{:S(2)}) copy-start(bf16[160,192]{1,0:T(8,128)(2,1)} %param.17) | copy-start | bytes 184324
  0.6 17.2 %copy-start.17 = (f32[2,1,1,6,3312]{4,2,3,1,0:T(1,128)S(1)}, f32[2,1,1,6,3312]{4,2,3,1,0:T(1,128)}, u32[]{:S(2)}) copy-start(f32[2,1,1,6,3312]{4,2,3,1,0:T(1,128)} %param.24) | copy-start | bytes 476932
  11.6 6.3 %copy-start.15 = (bf16[6,12,4,4,4]{1,4,3,2,0:T(4,128)(2,1)}, bf16[6,12,4,4,4]{1,4,3,2,0:T(4,128)(2,1)S(1)}, u32[]{:S(2)}) copy-start(bf16[6,12,4,4,4]{1,4,3,2,0:T(4,128)(2,1)S(1)} %copy.47) | copy-start | bytes 27652
  16.4 41.7 %copy-start.27 = (f32[1,1,192]{2,1,0:T(1,128)}, f32[1,1,192]{2,1,0:T(1,128)S(1)}, u32[]{:S(2)}) copy-start(f32[1,1,192]{2,1,0:T(1,128)S(1)} %get-tuple-element.41) | copy-start | bytes 2308
  16.4 55.7 %copy-start.32 = (f32[1,1,192]{2,1,0:T(1,128)}, f32[1,1,192]{2,1,0:T(1,128)S(1)}, u32[]{:S(2)}) copy-start(f32[1,1,192]{2,1,0:T(1,128)S(1)} %get-tuple-element.40) | copy-start | bytes 2308
  17.9 53.3 %copy-start.9 = (bf16[144,576]{0,1:T(8,128)(2,1)}, bf16[144,576]{0,1:T(8,128)(2,1)S(1)}, u32[]{:S(2)}) copy-start(bf16[144,576]{0,1:T(8,128)(2,1)S(1)} %copy.51) | copy-start | bytes 497668
  58.1 13.5 %copy-start.11 = (bf16[2,192,192]{2,1,0:T(8,128)(2,1)S(1)}, bf16[2,192,192]{2,1,0:T(8,128)(2,1)}, u32[]{:S(2)}) copy-start(bf16[2,192,192]{2,1,0:T(8,128)(2,1)} %param.21) | copy-start | bytes 442372
  69.7 4.5 %copy-start.5 = (bf16[2,768,192]{1,2,0:T(8,128)(2,1)S(1)}, bf16[2,768,192]{1,2,0:T(8,128)(2,1)}, u32[]{:S(2)}) copy-start(bf16[2,768,192]{1,2,0:T(8,128)(2,1)} %param.23) | copy-start | bytes 1769476
  69.8 12.3 %copy-start.22 = (bf16[2,6,12,192]{3,0,2,1:T(2,128)(2,1)S(1)}, bf16[2,6,12,192]{3,0,2,1:T(2,128)(2,1)}, u32[]{:S(2)}) copy-start(bf16[2,6,12,192]{3,0,2,1:T(2,128)(2,1)} %param.25) | copy-start | bytes 165892
  71.2 13.1 %copy-start.24 = (f32[6,144]{1,0:T(8,128)}, f32[6,144]{1,0:T(8,128)S(1)}, u32[]{:S(2)}) copy-start(f32[6,144]{1,0:T(8,128)S(1)} %get-tuple-element.47) | copy-start | bytes 10372
  71.9 12.4 %copy-start.29 = (f32[144]{0:T(256)}, f32[144]{0:T(256)S(1)}, u32[]{:S(2)}) copy-start(f32[144]{0:T(256)S(1)} %broadcast_multiply_fusion.3) | copy-start | bytes 1732
  72.1 2.1 copy-start.33
  72.1 2.1 copy-start.34
  74.2 9.5 %copy-start.13 = (f32[144,768]{1,0:T(8,128)}, f32[144,768]{1,0:T(8,128)S(1)}, u32[]{:S(2)}) copy-start(f32[144,768]{1,0:T(8,128)S(1)} %get-tuple-element.51) | copy-start | bytes 1327108
  74.2 9.5 %copy-start.14 = (f32[144,768]{1,0:T(8,128)}, f32[144,768]{1,0:T(8,128)S(1)}, u32[]{:S(2)}) copy-start(f32[144,768]{1,0:T(8,128)S(1)} %get-tuple-element.52) | copy-start | bytes 1327108
  75.2 59.5 %collective-permute-start.3 = (bf16[2,3,12,192]{3,2,1,0:T(8,128)(2,1)}, bf16[2,3,12,192]{3,2,1,0:T(8,128)(2,1)}, u32[]{:S(2)}, u32[]{:S(2)}) collective-permute-start(bf16[2,3,12,192]{3,2,1,0:T(8,128)(2,1)} %get-tuple-element.30), channel_id=1, source_target_pairs={{2,0},{4,2},{6,4},{8,6},{10,8},{12,10},{14,12},{0,14},{3,1},{5,3},... | collective-permute-start | bytes 82952 | tf_op jit(solution)/shard_map/ppermute | solution.py:16
  82.8 60.2 %collective-permute-start = (bf16[2,3,12,192]{3,0,2,1:T(2,128)(2,1)}, bf16[2,3,12,192]{3,0,2,1:T(2,128)(2,1)}, u32[]{:S(2)}, u32[]{:S(2)}) collective-permute-start(bf16[2,3,12,192]{3,0,2,1:T(2,128)(2,1)} %get-tuple-element.34), channel_id=1, source_target_pairs={{2,0},{4,2},{6,4},{8,6},{10,8},{12,10},{14,12},{0,14},{3,1},{5,3},... | collective-permute-start | bytes 82952 | tf_op jit(solution)/shard_map/ppermute | solution.py:16
  84.3 79.4 %copy-start.3 = (bf16[2,192,576]{2,1,0:T(8,128)(2,1)S(1)}, bf16[2,192,576]{2,1,0:T(8,128)(2,1)}, u32[]{:S(2)}) copy-start(bf16[2,192,576]{2,1,0:T(8,128)(2,1)} %param.20) | copy-start | bytes 1327108
  123.0 11.7 %copy-start.16 = (bf16[2,3,12,192]{3,2,1,0:T(8,128)(2,1)S(1)}, bf16[2,3,12,192]{3,2,1,0:T(8,128)(2,1)}, u32[]{:S(2)}) copy-start(bf16[2,3,12,192]{3,2,1,0:T(8,128)(2,1)} %get-tuple-element.29) | copy-start | bytes 82948
  123.0 19.9 %copy-start.18 = (bf16[2,3,12,192]{3,0,2,1:T(2,128)(2,1)S(1)}, bf16[2,3,12,192]{3,0,2,1:T(2,128)(2,1)}, u32[]{:S(2)}) copy-start(bf16[2,3,12,192]{3,0,2,1:T(2,128)(2,1)} %get-tuple-element.33) | copy-start | bytes 82948
  123.0 41.1 %copy-start.19 = (pred[144,144]{0,1:T(8,128)(4,1)S(1)}, pred[144,144]{0,1:T(8,128)(4,1)}, u32[]{:S(2)}) copy-start(pred[144,144]{0,1:T(8,128)(4,1)} %broadcast_compare_fusion) | copy-start | bytes 62212
  135.5 10.4 %collective-permute-start.4 = (bf16[1,6,12,192]{3,2,1,0:T(8,128)(2,1)S(1)}, bf16[1,6,12,192]{3,2,1,0:T(8,128)(2,1)S(1)}, u32[]{:S(2)}, u32[]{:S(2)}) collective-permute-start(bf16[1,6,12,192]{3,2,1,0:T(8,128)(2,1)S(1)} %get-tuple-element.28), channel_id=1, source_target_pairs={{1,0},{0,1},{3,2},{2,3},{5,4},{4,5},{7,6},{6,7},{9,8},{8,9},{11,10... | collective-permute-start | bytes 82952 | tf_op jit(solution)/shard_map/ppermute | solution.py:16
  143.9 9.8 %collective-permute-start.1 = (bf16[1,6,12,192]{3,0,2,1:T(2,128)(2,1)S(1)}, bf16[1,6,12,192]{3,0,2,1:T(2,128)(2,1)S(1)}, u32[]{:S(2)}, u32[]{:S(2)}) collective-permute-start(bf16[1,6,12,192]{3,0,2,1:T(2,128)(2,1)S(1)} %get-tuple-element.32), channel_id=1, source_target_pairs={{1,0},{0,1},{3,2},{2,3},{5,4},{4,5},{7,6},{6,7},{9,8},{8,9},{11,10... | collective-permute-start | bytes 82952 | tf_op jit(solution)/shard_map/ppermute | solution.py:16
  145.9 16.0 %collective-permute-start.5 = (bf16[2,6,6,192]{3,2,1,0:T(8,128)(2,1)S(1)}, bf16[2,6,6,192]{3,2,1,0:T(8,128)(2,1)S(1)}, u32[]{:S(2)}, u32[]{:S(2)}) collective-permute-start(bf16[2,6,6,192]{3,2,1,0:T(8,128)(2,1)S(1)} %get-tuple-element.26), channel_id=1, source_target_pairs={{16,0},{32,16},{48,32},{64,48},{80,64},{96,80},{112,96},{128,112},... | collective-permute-start | bytes 82952 | tf_op jit(solution)/shard_map/ppermute | solution.py:16
  154.6 12.9 %collective-permute-start.2 = (bf16[2,6,6,192]{3,0,2,1:T(2,128)(2,1)}, bf16[2,6,6,192]{3,0,2,1:T(2,128)(2,1)}, u32[]{:S(2)}, u32[]{:S(2)}) collective-permute-start(bf16[2,6,6,192]{3,0,2,1:T(2,128)(2,1)} %get-tuple-element.20), channel_id=1, source_target_pairs={{16,0},{32,16},{48,32},{64,48},{80,64},{96,80},{112,96},{128,112},... | collective-permute-start | bytes 82952 | tf_op jit(solution)/shard_map/ppermute | solution.py:16
  162.1 1.6 copy-start.20
  164.1 4.2 %copy-start.10 = (bf16[144,576]{0,1:T(8,128)(2,1)}, bf16[144,576]{0,1:T(8,128)(2,1)S(1)}, u32[]{:S(2)}) copy-start(bf16[144,576]{0,1:T(8,128)(2,1)S(1)} %copy.56) | copy-start | bytes 497668
  164.4 8.8 %copy-start.30 = (f32[1,1,192]{2,1,0:T(1,128)S(1)}, f32[1,1,192]{2,1,0:T(1,128)}, u32[]{:S(2)}) copy-start(f32[1,1,192]{2,1,0:T(1,128)} %get-tuple-element.39) | copy-start | bytes 2308
  164.5 9.3 %copy-start.12 = (bf16[2,192,192]{2,1,0:T(8,128)(2,1)S(1)}, bf16[2,192,192]{2,1,0:T(8,128)(2,1)}, u32[]{:S(2)}) copy-start(bf16[2,192,192]{2,1,0:T(8,128)(2,1)} %param.21) | copy-start | bytes 442372
  168.4 13.4 %copy-start.6 = (bf16[144,192]{1,0:T(8,128)(2,1)}, bf16[144,192]{1,0:T(8,128)(2,1)S(1)}, u32[]{:S(2)}) copy-start(bf16[144,192]{1,0:T(8,128)(2,1)S(1)} %reshape.642) | copy-start | bytes 165892
  170.8 12.0 %copy-start.21 = (f32[2,6,12]{2,1,0:T(8,128)S(1)}, f32[2,6,12]{2,1,0:T(8,128)}, u32[]{:S(2)}) copy-start(f32[2,6,12]{2,1,0:T(8,128)} %copy-done.20) | copy-start | bytes 1732
  173.3 12.0 %copy-start.26 = (f32[2,6,12]{2,1,0:T(8,128)S(1)}, f32[2,6,12]{2,1,0:T(8,128)}, u32[]{:S(2)}) copy-start(f32[2,6,12]{2,1,0:T(8,128)} %get-tuple-element.37) | copy-start | bytes 1732
  173.3 31.2 %copy-start.25 = (f32[2,6,12]{2,1,0:T(8,128)S(1)}, f32[2,6,12]{2,1,0:T(8,128)}, u32[]{:S(2)}) copy-start(f32[2,6,12]{2,1,0:T(8,128)} %get-tuple-element.35) | copy-start | bytes 1732
  173.8 9.1 %copy-start.31 = (f32[144]{0:T(256)}, f32[144]{0:T(256)S(1)}, u32[]{:S(2)}) copy-start(f32[144]{0:T(256)S(1)} %negate_multiply_fusion.7) | copy-start | bytes 1732
  175.4 44.9 %copy-start.1 = (f32[6,144,144]{1,2,0:T(8,128)S(1)}, f32[6,144,144]{1,2,0:T(8,128)}, u32[]{:S(2)}) copy-start(f32[6,144,144]{1,2,0:T(8,128)} %get-tuple-element.48) | copy-start | bytes 1492996
  183.9 43.8 %copy-start.4 = (bf16[2,192,576]{2,1,0:T(8,128)(2,1)S(1)}, bf16[2,192,576]{2,1,0:T(8,128)(2,1)}, u32[]{:S(2)}) copy-start(bf16[2,192,576]{2,1,0:T(8,128)(2,1)} %param.20) | copy-start | bytes 1327108
  188.2 42.6 %copy-start.2 = (bf16[3,6,12,5,2,4,4]{2,6,5,4,3,1,0:T(4,128)(2,1)S(1)}, bf16[3,6,12,5,2,4,4]{2,6,5,4,3,1,0:T(4,128)(2,1)}, u32[]{:S(2)}) copy-start(bf16[3,6,12,5,2,4,4]{2,6,5,4,3,1,0:T(4,128)(2,1)} %copy.49) | copy-start | bytes 207364
  188.2 8.9 %collective-permute-start.6 = (bf16[2,6,6,192]{3,2,1,0:T(8,128)(2,1)S(1)}, bf16[2,6,6,192]{3,2,1,0:T(8,128)(2,1)S(1)}, u32[]{:S(2)}, u32[]{:S(2)}) collective-permute-start(bf16[2,6,6,192]{3,2,1,0:T(8,128)(2,1)S(1)} %get-tuple-element.23), channel_id=1, source_target_pairs={{496,0},{0,16},{16,32},{32,48},{48,64},{64,80},{80,96},{96,112},{1... | collective-permute-start | bytes 82952 | tf_op jit(solution)/shard_map/ppermute | solution.py:16
  197.1 4.1 %collective-permute-start.7 = (bf16[2,3,12,192]{3,2,1,0:T(8,128)(2,1)S(1)}, bf16[2,3,12,192]{3,2,1,0:T(8,128)(2,1)S(1)}, u32[]{:S(2)}, u32[]{:S(2)}) collective-permute-start(bf16[2,3,12,192]{3,2,1,0:T(8,128)(2,1)S(1)} %fusion.216), channel_id=1, source_target_pairs={{14,0},{0,2},{2,4},{4,6},{6,8},{8,10},{10,12},{12,14},{15,1},{1,3}... | collective-permute-start | bytes 82952 | tf_op jit(solution)/shard_map/ppermute | solution.py:16
  201.2 8.7 %collective-permute-start.8 = (bf16[1,6,12,192]{3,2,1,0:T(8,128)(2,1)S(1)}, bf16[1,6,12,192]{3,2,1,0:T(8,128)(2,1)S(1)}, u32[]{:S(2)}, u32[]{:S(2)}) collective-permute-start(bf16[1,6,12,192]{3,2,1,0:T(8,128)(2,1)S(1)} %get-tuple-element.21), channel_id=1, source_target_pairs={{1,0},{0,1},{3,2},{2,3},{5,4},{4,5},{7,6},{6,7},{9,8},{8,9},{11,10... | collective-permute-start | bytes 82952 | tf_op jit(solution)/shard_map/ppermute | solution.py:16
  204.5 23.5 %copy-start.28 = (f32[144]{0:T(256)S(1)}, f32[144]{0:T(256)}, u32[]{:S(2)}) copy-start(f32[144]{0:T(256)} %div.130) | copy-start | bytes 1732
  210.0 0.6 copy-start.23
  211.5 3.9 %copy-start.7 = (bf16[144,192]{1,0:T(8,128)(2,1)}, bf16[144,192]{1,0:T(8,128)(2,1)S(1)}, u32[]{:S(2)}) copy-start(bf16[144,192]{1,0:T(8,128)(2,1)S(1)} %reshape.657) | copy-start | bytes 165892
  217.0 12.8 %copy-start.8 = (bf16[144,192]{1,0:T(8,128)(2,1)S(1)}, bf16[144,192]{1,0:T(8,128)(2,1)}, u32[]{:S(2)}) copy-start(bf16[144,192]{1,0:T(8,128)(2,1)} %copy-done.7) | copy-start | bytes 165892

commit v2 on v0

v2 whole, which is shorter than its diff:
```python
import functools

import jax
import jax.numpy as jnp
import numpy as np
from jax import lax
from jax.experimental import pallas as pl
from jax.experimental.pallas import tpu as pltpu
from jax.sharding import PartitionSpec as P

MESH = pl.DeviceIdType.MESH
f32 = jnp.float32
bf16 = jnp.bfloat16
norm_eps = 1e-05
HEADS = 6
TOKENS = 144
WIDTH = 192
FIELD_ROWS = 640
NN = (((1,), (0,)), ((), ()))
NT = (((1,), (1,)), ((), ()))
TN = (((0,), (0,)), ((), ()))


def dot(a, b, dims=NN):
    return lax.dot_general(a, b, dims, preferred_element_type=f32)


def tables():
    t = np.arange(TOKENS)
    col, level, row = t // 12, t // 6 % 2, t % 6
    octant = (col // 6) * 4 + level * 2 + row // 3
    place = octant * 32 + (col % 6) * 3 + row % 3
    tok_to_oct = np.zeros((256, TOKENS))
    tok_to_oct[place, t] = 1
    natural = (level * 6 + row) * 16 + col
    nat_to_oct = np.zeros((256, 192))
    nat_to_oct[place, natural] = 1
    tok_to_nat = np.zeros((192, TOKENS))
    tok_to_nat[natural, t] = 1
    pick = np.zeros((4, TOKENS, 48))
    for c in range(4):
        pick[c, t, 4 * col + c] = 1
    key_row = np.full((2, 1, FIELD_ROWS), -1.0)
    fold_upper = np.zeros((4, 256, 160))
    fold_surface = np.zeros((4, 128, 64))
    for v in range(5):
        for a in range(2):
            for y in range(24):
                r = (v * 2 + a) * 24 + y
                key_row[1, 0, r] = y // 4
                key_row[:, 0, 256 + r] = 8 + y // 4
                for c in range(4):
                    fold_upper[c, r, v * 32 + a * 16 + (y % 4) * 4 + c] = 1
    for v in range(4):
        for y in range(24):
            r = v * 24 + y
            key_row[0, 0, 512 + r] = y // 4
            for c in range(4):
                fold_surface[c, r, v * 16 + (y % 4) * 4 + c] = 1
    key_tok = (level * 8 + row).reshape(TOKENS, 1)
    spread = np.zeros((2, 138, 276))
    for z in range(2):
        for a in range(6):
            for k in range(23):
                spread[z, a * 23 + k, (22 - k) * 12 + z * 6 + a] = 1
    heads = np.zeros((HEADS, 1, WIDTH))
    for h in range(HEADS):
        heads[h, 0, 32 * h : 32 * h + 32] = 1
    place_col = np.stack((level, row // 3)).reshape(2, TOKENS, 1)
    place_row = np.stack((level, row // 3)).reshape(2, 1, TOKENS)
    return {
        "tok_to_oct": tok_to_oct.astype(jnp.bfloat16),
        "oct_to_tok": tok_to_oct.T.astype(jnp.bfloat16),
        "nat_to_oct": nat_to_oct.astype(jnp.bfloat16),
        "tok_to_nat": tok_to_nat.astype(jnp.bfloat16),
        "pick": pick.astype(jnp.bfloat16),
        "key_row": key_row.astype(np.float32),
        "key_tok": key_tok.astype(np.float32),
        "fold_upper": fold_upper.astype(jnp.bfloat16),
        "fold_surface": fold_surface.astype(jnp.bfloat16),
        "spread": spread.astype(jnp.bfloat16),
        "heads": heads.astype(np.float32),
        "place_col": place_col.astype(np.float32),
        "place_row": place_row.astype(np.float32),
    }


def centre(values):
    average = jnp.mean(values, -1, keepdims=True)
    centred = values - average
    variance = jnp.mean(centred * centred, -1, keepdims=True)
    scale = lax.rsqrt(variance + norm_eps)
    return centred * scale, scale


def norm_backward(unit, scale, gain, cotangent):
    scaled = cotangent * gain
    first = jnp.mean(scaled, -1, keepdims=True)
    second = jnp.mean(scaled * unit, -1, keepdims=True)
    return scale * (scaled - first - unit * second)


def build_bias(table_ref, spread_ref, tab, strip, bias):
    for z in range(2):
        for zt in range(2):
            for a in range(6):
                start = ((zt * 2 + z) * 6 + a) * 138
                tab[z, (zt * 6 + a) * 8 : (zt * 6 + a) * 8 + 6, :] = table_ref[:, start : start + 138]
    total = None
    for z in range(2):
        rest = tab[z]
        for part in range(3):
            piece = rest.astype(bf16)
            rest = rest - piece.astype(f32)
            term = dot(piece, spread_ref[z])
            total = term if total is None else total + term
    strip[...] = total
    for h in range(HEADS):
        lines = jnp.concatenate([strip[8 * k + h : 8 * k + h + 1, :] for k in range(12)], 0)
        for o in range(12):
            bias[h, 12 * o : 12 * o + 12, :] = lines[:, 12 * (11 - o) : 12 * (11 - o) + TOKENS]


def block_forward(x, b, w, bias, saved, final):
    gains, qkv_w, proj_w, up_w, down_w, heads = w
    unit0, scale0 = centre(x)
    hidden = (unit0 * gains[b, 0:1, :]).astype(bf16)
    qkv = dot(hidden, qkv_w[b]).astype(bf16)
    saved["qkv"][b] = qkv
    query = qkv[:, :WIDTH]
    key = qkv[:, WIDTH : 2 * WIDTH]
    value = qkv[:, 2 * WIDTH :]
    mixed = None
    for h in range(HEADS):
        head = heads[h]
        score = dot(query * head.astype(bf16), key, NT) * 32 ** (-0.5) + bias[h]
        expo = jnp.exp(score - jnp.max(score, -1, keepdims=True))
        prob = expo / jnp.sum(expo, -1, keepdims=True)
        saved["prob"][b, h] = prob
        part = dot(prob.astype(bf16), value) * head
        mixed = part if mixed is None else mixed + part
    resid = x + dot(mixed.astype(bf16), proj_w[b])
    unit1, scale1 = centre(resid)
    normed = (unit1 * gains[b, 1:2, :]).astype(bf16)
    upward = dot(normed, up_w[b])
    saved["unit0"][b] = unit0
    saved["scale0"][b] = scale0
    saved["unit1"][b] = unit1
    saved["scale1"][b] = scale1
    saved["upward"][b] = upward
    if final:
        return None
    active = 0.5 * upward * (1.0 + lax.erf(upward * 2 ** (-0.5)))
    return resid + dot(active.astype(bf16), down_w[b])


def gelu_slope(b, saved):
    upward = saved["upward"][b]
    slope = 0.5 * (1.0 + lax.erf(upward * 2 ** (-0.5)))
    saved["slope"][...] = slope + upward * jnp.exp(-0.5 * upward * upward) * (2 * np.pi) ** (-0.5)


def block_backward(dout, b, w, saved):
    gains, qkv_w, proj_w, up_w, down_w, heads = w
    dactive = dot(dout.astype(bf16), down_w[b], NT).astype(bf16).astype(f32)
    dupward = dactive * saved["slope"][...]
    dnormed = dot(dupward.astype(bf16), up_w[b], NT).astype(bf16).astype(f32)
    dresid = dout + norm_backward(saved["unit1"][b], saved["scale1"][b], gains[b, 1:2, :], dnormed)
    dmixed = dot(dresid.astype(bf16), proj_w[b], NT).astype(bf16)
    qkv = saved["qkv"][b]
    query = qkv[:, :WIDTH]
    key = qkv[:, WIDTH : 2 * WIDTH]
    value = qkv[:, 2 * WIDTH :]
    dquery = dkey = dvalue = None
    for h in range(HEADS):
        head = heads[h]
        narrow = head.astype(bf16)
        prob = saved["prob"][b, h]
        dmixed_h = dmixed * narrow
        dweights = dot(dmixed_h, value, NT).astype(bf16).astype(f32)
        dv = dot(prob.astype(bf16), dmixed_h, TN)
        inner = jnp.sum(dweights * prob, -1, keepdims=True)
        dscore = (prob * (dweights - inner) * 32 ** (-0.5)).astype(bf16)
        dq = dot(dscore, key) * head
        dk = dot(dscore, query * narrow, TN)
        dquery = dq if dquery is None else dquery + dq
        dkey = dk if dkey is None else dkey + dk
        dvalue = dv if dvalue is None else dvalue + dv
    dqkv = jnp.concatenate((dquery, dkey, dvalue), 1).astype(bf16)
    dhidden = dot(dqkv, qkv_w[b], NT).astype(bf16).astype(f32)
    return dresid + norm_backward(saved["unit0"][b], saved["scale0"][b], gains[b, 0:1, :], dhidden)


def wait_bytes(buffer, start, count, sem):
    view = buffer.at[pl.ds(start, count)]
    pltpu.make_async_copy(view, view, sem).wait()


def send_octants(src, dst, send_sem, recv_sem, forward):
    lon_count, lat_count = lax.axis_size("lon"), lax.axis_size("lat")
    lon, lat, section = lax.axis_index("lon"), lax.axis_index("lat"), lax.axis_index("section")
    for k in range(8):
        step = tuple((1 - (k >> bit & 1)) if forward else (k >> bit & 1) for bit in (2, 1, 0))
        if step == (0, 0, 0):
            dst[7 - k] = src[k]
            continue
        sign = -1 if forward else 1
        target = {}
        if step[0]:
            target["lon"] = lax.rem(lon + sign + lon_count, lon_count)
        if step[1]:
            target["section"] = 1 - section
        if step[2]:
            target["lat"] = lax.rem(lat + sign + lat_count, lat_count)
        pltpu.make_async_remote_copy(
            src_ref=src.at[k],
            dst_ref=dst.at[7 - k],
            send_sem=send_sem,
            recv_sem=recv_sem,
            device_id=target,
            device_id_type=MESH,
        ).start()


def whole_kernel(names, owners, unit, *refs):
    consts = dict(zip(names, refs))
    (
        upper_ref,
        surface_ref,
        upper_embed,
        surface_embed,
        gains,
        qkv_w,
        proj_w,
        up_w,
        down_w,
        table_ref,
        grad_ref,
        latent_out,
        upper_out,
        surface_out,
        field,
        natural,
        tab,
        strip,
        bias0,
        bias1,
        qkv_s,
        prob_s,
        unit0_s,
        scale0_s,
        unit1_s,
        scale1_s,
        upward_s,
        slope_s,
        patch_upper,
        patch_surface,
        grad_send,
        grad_recv,
        x_send,
        x_recv,
        back_send,
        back_recv,
        terms,
        held,
        piece,
        across,
        last,
        result,
        sems,
    ) = refs[len(names) :]
    lon_count = lax.axis_size("lon")
    lat_count = lax.axis_size("lat")
    section_count = lax.axis_size("section")
    lon = lax.axis_index("lon")
    lat = lax.axis_index("lat")
    section = lax.axis_index("section")
    group = lat_count * section_count
    mine = section * lat_count + lat
    barrier = pltpu.get_barrier_semaphore()

    def peer_of(d):
        other = lax.rem(mine + d, group)
        return {"lat": lax.rem(other, lat_count), "section": other // lat_count}

    def greet_lon(d, carry):
        pl.semaphore_signal(
            barrier, inc=1, device_id={"lon": lax.rem(lon + d, lon_count)}, device_id_type=MESH
        )
        return carry

    def greet_group(d, carry):
        pl.semaphore_signal(barrier, inc=1, device_id=peer_of(d), device_id_type=MESH)
        return carry

    for sign in (-1, 1):
        lon_next = lax.rem(lon + sign + lon_count, lon_count)
        lat_next = lax.rem(lat + sign + lat_count, lat_count)
        for target in (
            {"lon": lon_next, "section": 1 - section},
            {"lon": lon_next, "lat": lat_next},
            {"lon": lon_next, "lat": lat_next, "section": 1 - section},
        ):
            pl.semaphore_signal(barrier, inc=1, device_id=target, device_id_type=MESH)
    lax.fori_loop(1, lon_count, greet_lon, 0)
    lax.fori_loop(1, group, greet_group, 0)

    natural[...] = jnp.zeros_like(natural)
    for z in range(2):
        for a in range(6):
            natural[z * 6 + a, 0:12, :] = grad_ref[z, a].astype(f32)
    octants = dot(consts["nat_to_oct"][...], natural[...].reshape(192, WIDTH).astype(bf16))
    grad_send[...] = octants.astype(bf16).reshape(8, 32, WIDTH)

    field[240:256, :] = jnp.zeros((16, 48), f32)
    field[496:512, :] = jnp.zeros((16, 48), f32)
    field[608:640, :] = jnp.zeros((32, 48), f32)
    for v in range(5):
        for a in range(2):
            row = (v * 2 + a) * 24
            field[row : row + 24, :] = upper_ref[v, 2 + a].astype(f32)
            field[256 + row : 256 + row + 24, :] = upper_ref[v, 4 * section + a].astype(f32)
    for v in range(4):
        field[512 + 24 * v : 512 + 24 * v + 24, :] = surface_ref[v].astype(f32)
    fields = field[...].astype(bf16)
    same = consts["key_tok"][...] == consts["key_row"][section]
    upper_total = surface_total = None
    for c in range(4):
        spreads = jnp.where(same, dot(consts["pick"][c], fields, NT), 0.0)
        upper_c = (spreads[:, :256] + spreads[:, 256:512]).astype(bf16)
        surface_c = spreads[:, 512:].astype(bf16)
        upper_c = dot(upper_c, consts["fold_upper"][c])
        surface_c = dot(surface_c, consts["fold_surface"][c])
        upper_total = upper_c if upper_total is None else upper_total + upper_c
        surface_total = surface_c if surface_total is None else surface_total + surface_c
    patch_upper[...] = upper_total.astype(bf16)
    patch_surface[...] = surface_total.astype(bf16)
    latent = dot(patch_upper[...], upper_embed[...]) + dot(patch_surface[...], surface_embed[...])
    latent = latent.astype(bf16).astype(f32)
    build_bias(table_ref.at[0], consts["spread"], tab, strip, bias0)

    pl.semaphore_wait(barrier, lon_count - 1 + group - 1 + 6)
    send_octants(grad_send, grad_recv, sems.at[0], sems.at[1], True)

    w = (gains, qkv_w, proj_w, up_w, down_w, consts["heads"])
    saved = {
        "qkv": qkv_s,
        "prob": prob_s,
        "unit0": unit0_s,
        "scale0": scale0_s,
        "unit1": unit1_s,
        "scale1": scale1_s,
        "upward": upward_s,
        "slope": slope_s,
    }
    first = block_forward(latent, 0, w, bias0, saved, False)
    octants = dot(consts["tok_to_oct"][...], first.astype(bf16))
    x_send[...] = octants.astype(bf16).reshape(8, 32, WIDTH)
    send_octants(x_send, x_recv, sems.at[2], sems.at[3], True)

    build_bias(table_ref.at[1], consts["spread"], tab, strip, bias1)
    last_section = (section == section_count - 1).astype(f32)
    last_band = (lat == lat_count - 1).astype(f32)
    apart = jnp.abs(consts["place_col"][0] - consts["place_row"][0]) * last_section
    apart = apart + jnp.abs(consts["place_col"][1] - consts["place_row"][1]) * last_band
    for h in range(HEADS):
        bias1[h] = jnp.where(apart > 0.5, -1e30, bias1[h])
    wait_bytes(grad_recv, 1, 7, sems.at[1])
    dshifted = dot(consts["oct_to_tok"][...], grad_recv[...].reshape(256, WIDTH))
    wait_bytes(x_recv, 1, 7, sems.at[3])
    shifted = dot(consts["oct_to_tok"][...], x_recv[...].reshape(256, WIDTH))

    block_forward(shifted, 1, w, bias1, saved, True)
    gelu_slope(1, saved)
    dmiddle = block_backward(dshifted, 1, w, saved)
    octants = dot(consts["tok_to_oct"][...], dmiddle.astype(bf16))
    back_send[...] = octants.astype(bf16).reshape(8, 32, WIDTH)
    send_octants(back_send, back_recv, sems.at[4], sems.at[5], False)
    gelu_slope(0, saved)
    wait_bytes(back_recv, 0, 7, sems.at[5])
    dfirst = dot(consts["oct_to_tok"][...], back_recv[...].reshape(256, WIDTH))
    dlatent = block_backward(dfirst, 0, w, saved).astype(bf16)

    upper_terms = dot(patch_upper[...], dlatent, TN)
    surface_terms = dot(patch_surface[...], dlatent, TN)
    both = jnp.concatenate((upper_terms, surface_terms), 0)
    terms[0:14, :, :] = both[:, :128].astype(bf16).reshape(14, 16, 128)
    low = both[:, 128:]
    low = jnp.concatenate((low[:112], low[112:]), 1)
    terms[14:21, :, :] = low.astype(bf16).reshape(7, 16, 128)

    def scatter(d, carry):
        peer = lax.rem(lon + d, lon_count)

        @pl.when(peer < owners)
        def _():
            pltpu.make_async_remote_copy(
                src_ref=terms.at[pl.ds(peer * unit, unit)],
                dst_ref=held.at[pl.ds((d - 1) * unit, unit)],
                send_sem=sems.at[6],
                recv_sem=sems.at[7],
                device_id={"lon": peer},
                device_id_type=MESH,
            ).start()

        return carry

    lax.fori_loop(1, lon_count, scatter, 0)

    grads = dot(consts["tok_to_nat"][...], dlatent).astype(bf16)
    for z in range(2):
        for a in range(6):
            k = (z * 6 + a) * 16
            latent_out[z, a] = grads[k : k + 16][:12]

    @pl.when(lon < owners)
    def _():
        wait_bytes(held, 0, (lon_count - 1) * unit, sems.at[7])
        total = terms[pl.ds(lon * unit, unit)].astype(f32)
        for d in range(lon_count - 1):
            total = total + held[d * unit : d * unit + unit].astype(f32)
        piece[...] = total.astype(bf16)
        across[pl.ds(mine * unit, unit)] = total.astype(bf16)

        def exchange(d, carry):
            pltpu.make_async_remote_copy(
                src_ref=piece,
                dst_ref=across.at[pl.ds(mine * unit, unit)],
                send_sem=sems.at[8],
                recv_sem=sems.at[9],
                device_id=peer_of(d),
                device_id_type=MESH,
            ).start()
            return carry

        lax.fori_loop(1, group, exchange, 0)
        wait_bytes(across, 0, (group - 1) * unit, sems.at[9])
        whole = across[0:unit].astype(f32)
        for d in range(1, group):
            whole = whole + across[d * unit : d * unit + unit].astype(f32)
        last[...] = whole.astype(bf16)
        result[pl.ds(lon * unit, unit)] = whole.astype(bf16)

        def gather(d, carry):
            pltpu.make_async_remote_copy(
                src_ref=last,
                dst_ref=result.at[pl.ds(lon * unit, unit)],
                send_sem=sems.at[10],
                recv_sem=sems.at[11],
                device_id={"lon": lax.rem(lon + d, lon_count)},
                device_id_type=MESH,
            ).start()
            return carry

        lax.fori_loop(1, lon_count, gather, 0)
        wait_bytes(terms, 0, (owners - 1) * unit, sems.at[6])
        wait_bytes(across, 0, (group - 1) * unit, sems.at[8])
        wait_bytes(result, 0, (owners - 1) * unit, sems.at[11])
        wait_bytes(held, 0, (lon_count - 1) * unit, sems.at[10])

    @pl.when(lon >= owners)
    def _():
        wait_bytes(terms, 0, owners * unit, sems.at[6])
        wait_bytes(result, 0, owners * unit, sems.at[11])

    scale = float(4 * 6 * lat_count * 12 * lon_count) ** (-0.5)
    high = result[0:14].astype(f32).reshape(224, 128) * scale
    low = result[14:21].astype(f32).reshape(112, 128) * scale
    upper_out[:, 0:128] = high[:160]
    surface_out[:, 0:128] = high[160:]
    upper_out[0:112, 128:192] = low[:, :64]
    upper_out[112:160, 128:192] = low[:48, 64:]
    surface_out[:, 128:192] = low[48:, 64:]
    wait_bytes(grad_send, 0, 7, sems.at[0])
    wait_bytes(x_send, 0, 7, sems.at[2])
    wait_bytes(back_send, 0, 7, sems.at[4])


def on_device(
    upper_fields,
    surface_fields,
    upper_embed,
    surface_embed,
    norm_gains,
    qkv_weight,
    proj_weight,
    up_weight,
    down_weight,
    earth_bias,
    out_grad,
):
    consts = tables()
    names = tuple(consts)
    lon_count = lax.axis_size("lon")
    group = lax.axis_size("lat") * lax.axis_size("section")
    unit = -(-21 // lon_count)
    owners = -(-21 // unit)
    vmem = pl.BlockSpec(memory_space=pltpu.VMEM)
    return pl.pallas_call(
        functools.partial(whole_kernel, names, owners, unit),
        out_shape=(
            jax.ShapeDtypeStruct(out_grad.shape, bf16),
            jax.ShapeDtypeStruct((160, WIDTH), f32),
            jax.ShapeDtypeStruct((64, WIDTH), f32),
        ),
        in_specs=[vmem] * (len(names) + 11),
        out_specs=(vmem,) * 3,
        scratch_shapes=[
            pltpu.VMEM((FIELD_ROWS, 48), f32),
            pltpu.VMEM((12, 16, WIDTH), f32),
            pltpu.VMEM((2, 96, 138), f32),
            pltpu.VMEM((96, 276), f32),
            pltpu.VMEM((HEADS, TOKENS, TOKENS), f32),
            pltpu.VMEM((HEADS, TOKENS, TOKENS), f32),
            pltpu.VMEM((2, TOKENS, 3 * WIDTH), bf16),
            pltpu.VMEM((2, HEADS, TOKENS, TOKENS), f32),
            pltpu.VMEM((2, TOKENS, WIDTH), f32),
            pltpu.VMEM((2, TOKENS, 1), f32),
            pltpu.VMEM((2, TOKENS, WIDTH), f32),
            pltpu.VMEM((2, TOKENS, 1), f32),
            pltpu.VMEM((2, TOKENS, 768), f32),
            pltpu.VMEM((TOKENS, 768), f32),
            pltpu.VMEM((TOKENS, 160), bf16),
            pltpu.VMEM((TOKENS, 64), bf16),
            pltpu.VMEM((8, 32, WIDTH), bf16),
            pltpu.VMEM((8, 32, WIDTH), bf16),
            pltpu.VMEM((8, 32, WIDTH), bf16),
            pltpu.VMEM((8, 32, WIDTH), bf16),
            pltpu.VMEM((8, 32, WIDTH), bf16),
            pltpu.VMEM((8, 32, WIDTH), bf16),
            pltpu.VMEM((owners * unit, 16, 128), bf16),
            pltpu.VMEM(((lon_count - 1) * unit, 16, 128), bf16),
            pltpu.VMEM((unit, 16, 128), bf16),
            pltpu.VMEM((group * unit, 16, 128), bf16),
            pltpu.VMEM((unit, 16, 128), bf16),
            pltpu.VMEM((owners * unit, 16, 128), bf16),
            pltpu.SemaphoreType.DMA((12,)),
        ],
        compiler_params=pltpu.CompilerParams(
            collective_id=0, has_side_effects=True, vmem_limit_bytes=48 * 2**20
        ),
    )(
        *consts.values(),
        upper_fields,
        surface_fields,
        upper_embed,
        surface_embed,
        norm_gains,
        qkv_weight,
        proj_weight,
        up_weight,
        down_weight,
        earth_bias.reshape(2, HEADS, -1),
        out_grad,
    )


def solution(mesh):
    placed = (
        P(None, None, "lat", "lon"),
        P(None, "lat", "lon"),
        P(),
        P(),
        P(),
        P(),
        P(),
        P(),
        P(),
        P(None, "lat", "section", None, None),
        P("section", "lat", "lon", None),
    )
    return jax.shard_map(
        on_device,
        mesh=mesh,
        in_specs=placed,
        out_specs=(P("section", "lat", "lon", None), P(), P()),
        check_vma=False,
    )
```

time: 607 us -> 78.1 us (0.13)
  waiting for transfers between devices: 268 us -> 0 us
  local copies, waits for them, and re-layouts: 125 us -> 16.4 us
  blocking collectives: 96.8 us -> 0 us
  Pallas kernels: 0 us -> 60.3 us
  starting transfers between devices: 38.4 us -> 0 us
  matrix products: 37.3 us -> 0 us
  other arithmetic: 25.4 us -> 0 us
  between operations: 14.8 us -> 0.8 us
    psum x1 -> x0, waiting for transfers between devices: 255 us -> none  [on_device(): lax.psum((upper_terms, surface_terms), ('lon', 'lat', 'section'))]
    gather x4 -> x0, local copies, waits for them, and re-layouts: 101 us -> none  [window_bias(): return table[..., bias_index()]]
    psum x1 -> x0, blocking collectives: 96.8 us -> none  [on_device(): lax.psum((upper_terms, surface_terms), ('lon', 'lat', 'section'))]
    pallas_call x0 -> x1, Pallas kernels: none -> 60.3 us  [on_device(): pl.pallas_call(functools.partial(whole_kernel, names, owners, unit), out_...]
    ppermute x9 -> x0, starting transfers between devices: 38.4 us -> none  [shifted(): return lax.ppermute(block, axis, route)]
    dot_general x31 -> x0, matrix products: 37.3 us -> none  [the longest x2 4.76 us: attention_backward(): jnp.einsum('zlwhqk,zlwqhd->zlwkhd', dscore, query.astype(jnp.float32), pr...]
    ppermute x9 -> x0, waiting for transfers between devices: 12.8 us -> none  [shifted(): return lax.ppermute(block, axis, route)]
    unnamed x55 -> x47, local copies, waits for them, and re-layouts: 4.19 us -> 15.6 us
  transfers between devices with their start and end apart: 10 -> 0, of which waited for: 4 -> 0; matrix products, arithmetic and copies ran while one was open for 12% -> 0% of each run, Pallas kernels for 0% -> 0%
where the time goes in v2:
time: 78.1 us; the launch traced here: 77.5 us
  Pallas kernels  60.3 us (77%)
  local copies, waits for them, and re-layouts  16.4 us (21%)
  between operations  0.8 us (1%)
    pallas_call x1, Pallas kernels, on_device(): pl.pallas_call(functools.partial(whole_kernel, names, owners, unit), out_...  60.3 us
    unnamed x47, local copies, waits for them, and re-layouts  15.6 us

profile of v2, /device:TPU:1, one launch (start us, length us, event | category | flops | bytes accessed | tf_op | source)
XLA Modules:
  0.0 77.5 jit_solution(18125595752808628409)
XLA Ops:
  0.6 0.0 copy-start.20
  0.6 0.0 copy-start.5
  0.7 0.9 %copy.33.refs_23_ = bf16[2,6,12,192]{3,2,1,0:T(8,128)(2,1)S(1)} copy(bf16[2,6,12,192]{3,0,2,1:T(2,128)(2,1)} %param.34) | data formatting | bytes 110592 | tf_op args[10]
  1.6 0.0 copy-start.3
  1.6 0.0 copy-start.4
  1.6 1.0 %copy.36 = f32[2,1,1,6,3312]{4,0,3,2,1:T(2,128)S(1)} copy(f32[2,1,1,6,3312]{4,2,3,1,0:T(1,128)} %param.33) | data formatting | bytes 317952 | tf_op args[9]
  2.7 0.0 copy-start.2
  2.7 0.0 copy-start
  2.7 0.0 copy-start.1
  2.7 0.0 copy-start.15
  2.8 1.4 %copy.31.refs_21_ = bf16[2,768,192]{2,1,0:T(8,128)(2,1)S(1)} copy(bf16[2,768,192]{1,2,0:T(8,128)(2,1)} %param.32) | data formatting | bytes 1179648 | tf_op args[8]
  4.2 0.0 copy-done.20
  4.2 0.0 copy-done.5
  4.2 0.0 copy-done.3
  4.2 0.0 copy-done.4
  4.2 0.0 copy-done.2
  4.3 0.0 copy-done
  4.3 0.0 copy-done.1
  4.3 0.0 copy-done.15
  4.3 0.0 copy-start.6
  4.3 0.9 %copy-done.6 = f32[2,144,1]{2,1,0:T(8,128)S(1)} copy-done((f32[2,144,1]{2,1,0:T(8,128)S(1)}, f32[2,144,1]{2,1,0:T(8,128)}, u32[]{:S(2)}) %copy-start.6) | copy-done | bytes 1176
  5.2 0.0 copy-start.7
  5.2 0.9 %copy-done.7 = bf16[4,144,48]{2,1,0:T(8,128)(2,1)S(1)} copy-done((bf16[4,144,48]{2,1,0:T(8,128)(2,1)S(1)}, bf16[4,144,48]{2,1,0:T(8,128)(2,1)}, u32[]{:S(2)}) %copy-start.7) | copy-done | bytes 55320
  6.1 0.0 copy-start.8
  6.1 0.9 %copy-done.8 = bf16[4,128,64]{2,1,0:T(8,128)(2,1)S(1)} copy-done((bf16[4,128,64]{2,1,0:T(8,128)(2,1)S(1)}, bf16[4,128,64]{2,1,0:T(8,128)(2,1)}, u32[]{:S(2)}) %copy-start.8) | copy-done | bytes 65560
  7.0 0.0 copy-start.9
  7.0 0.9 %copy-done.9 = bf16[256,192]{1,0:T(8,128)(2,1)S(1)} copy-done((bf16[256,192]{1,0:T(8,128)(2,1)S(1)}, bf16[256,192]{1,0:T(8,128)(2,1)}, u32[]{:S(2)}) %copy-start.9) | copy-done | bytes 98328
  7.9 0.0 copy-start.10
  7.9 0.9 %copy-done.10 = bf16[256,144]{1,0:T(8,128)(2,1)S(1)} copy-done((bf16[256,144]{1,0:T(8,128)(2,1)S(1)}, bf16[256,144]{1,0:T(8,128)(2,1)}, u32[]{:S(2)}) %copy-start.10) | copy-done | bytes 73752
  8.8 0.0 copy-start.11
  8.8 0.9 %copy-done.11 = bf16[192,144]{1,0:T(8,128)(2,1)S(1)} copy-done((bf16[192,144]{1,0:T(8,128)(2,1)S(1)}, bf16[192,144]{1,0:T(8,128)(2,1)}, u32[]{:S(2)}) %copy-start.11) | copy-done | bytes 55320
  9.7 0.0 copy-start.12
  9.7 0.9 %copy-done.12 = bf16[160,192]{1,0:T(8,128)(2,1)S(1)} copy-done((bf16[160,192]{1,0:T(8,128)(2,1)S(1)}, bf16[160,192]{1,0:T(8,128)(2,1)}, u32[]{:S(2)}) %copy-start.12) | copy-done | bytes 61464
  10.6 0.0 copy-start.13
  10.6 0.9 %copy-done.13 = f32[144,1]{1,0:T(8,128)S(1)} copy-done((f32[144,1]{1,0:T(8,128)S(1)}, f32[144,1]{1,0:T(8,128)}, u32[]{:S(2)}) %copy-start.13) | copy-done | bytes 600
  11.5 0.0 copy-start.14
  11.5 0.9 %copy-done.14 = bf16[144,256]{1,0:T(8,128)(2,1)S(1)} copy-done((bf16[144,256]{1,0:T(8,128)(2,1)S(1)}, bf16[144,256]{1,0:T(8,128)(2,1)}, u32[]{:S(2)}) %copy-start.14) | copy-done | bytes 73752
  12.4 0.0 copy-start.16
  12.4 0.7 copy-done.16
  13.1 0.0 copy-start.17
  13.1 0.7 copy-done.17
  13.8 0.0 copy-start.18
  13.8 0.7 copy-done.18
  14.5 0.0 copy-start.19
  14.5 0.7 copy-done.19
  15.2 60.3 %shard_map.247 = (bf16[2,6,12,192]{3,2,1,0:T(8,128)(2,1)S(1)}, f32[160,192]{1,0:T(8,128)S(1)}, f32[64,192]{1,0:T(8,128)S(1)}) custom-call(bf16[256,144]{1,0:T(8,128)(2,1)S(1)} %copy-done.10, bf16[144,256]{1,0:T(8,128)(2,1)S(1)} %copy-done.14, bf16[256,192]{1,0:T(8,128)(2,1)S(1)} %copy-done.9, bf16[192,144]{1,0:T(8,128)(2,1)S(1)} %copy-done.11, ...), custom_call_target="tpu_custom_call" | custom-call | tf_op jit(solution)/shard_map/pallas_call | solution.py:499
  75.5 0.7 copy.34
  76.2 0.7 copy.39
  76.9 0.6 copy.40
  (1 shorter events, 0.0 us)
Async XLA Ops:
  0.6 3.6 %copy-start.20 = (f32[2,1,144]{2,1,0:T(1,128)S(1)}, f32[2,1,144]{2,1,0:T(1,128)}, u32[]{:S(2)}) copy-start(f32[2,1,144]{2,1,0:T(1,128)} %constant.38.clone.refs_12_) | copy-start | bytes 3460
  0.6 3.6 %copy-start.5 = (bf16[5,6,24,48]{3,2,1,0:T(8,128)(2,1)S(1)}, bf16[5,6,24,48]{3,2,1,0:T(8,128)(2,1)}, u32[]{:S(2)}) copy-start(bf16[5,6,24,48]{3,2,1,0:T(8,128)(2,1)} %refs_13_.1) | copy-start | bytes 207364
  1.6 2.6 %copy-start.3 = (bf16[2,138,276]{2,1,0:T(8,128)(2,1)S(1)}, bf16[2,138,276]{2,1,0:T(8,128)(2,1)}, u32[]{:S(2)}) copy-start(bf16[2,138,276]{2,1,0:T(8,128)(2,1)} %constant.35.clone.refs_9_) | copy-start | bytes 457060
  1.6 2.6 %copy-start.4 = (bf16[2,192,192]{2,1,0:T(8,128)(2,1)S(1)}, bf16[2,192,192]{2,1,0:T(8,128)(2,1)}, u32[]{:S(2)}) copy-start(bf16[2,192,192]{2,1,0:T(8,128)(2,1)} %refs_19_.1) | copy-start | bytes 442372
  2.7 1.6 %copy-start.2 = (bf16[2,192,576]{2,1,0:T(8,128)(2,1)S(1)}, bf16[2,192,576]{2,1,0:T(8,128)(2,1)}, u32[]{:S(2)}) copy-start(bf16[2,192,576]{2,1,0:T(8,128)(2,1)} %refs_18_.1) | copy-start | bytes 1327108
  2.7 1.5 %copy-start = (bf16[2,192,768]{2,1,0:T(8,128)(2,1)S(1)}, bf16[2,192,768]{2,1,0:T(8,128)(2,1)}, u32[]{:S(2)}) copy-start(bf16[2,192,768]{2,1,0:T(8,128)(2,1)} %refs_20_.1) | copy-start | bytes 1769476
  2.7 1.5 %copy-start.1 = (bf16[4,256,160]{2,1,0:T(8,128)(2,1)S(1)}, bf16[4,256,160]{2,1,0:T(8,128)(2,1)}, u32[]{:S(2)}) copy-start(bf16[4,256,160]{2,1,0:T(8,128)(2,1)} %constant.33.clone.refs_7_) | copy-start | bytes 983044
  2.7 1.5 %copy-start.15 = (bf16[64,192]{1,0:T(8,128)(2,1)S(1)}, bf16[64,192]{1,0:T(8,128)(2,1)}, u32[]{:S(2)}) copy-start(bf16[64,192]{1,0:T(8,128)(2,1)} %refs_16_.1) | copy-start | bytes 73732
  4.3 0.9 %copy-start.6 = (f32[2,144,1]{2,1,0:T(8,128)S(1)}, f32[2,144,1]{2,1,0:T(8,128)}, u32[]{:S(2)}) copy-start(f32[2,144,1]{2,1,0:T(8,128)} %constant.37.clone.refs_11_) | copy-start | bytes 3460
  5.2 0.9 %copy-start.7 = (bf16[4,144,48]{2,1,0:T(8,128)(2,1)S(1)}, bf16[4,144,48]{2,1,0:T(8,128)(2,1)}, u32[]{:S(2)}) copy-start(bf16[4,144,48]{2,1,0:T(8,128)(2,1)} %constant.30.clone.refs_4_) | copy-start | bytes 165892
  6.1 0.9 %copy-start.8 = (bf16[4,128,64]{2,1,0:T(8,128)(2,1)S(1)}, bf16[4,128,64]{2,1,0:T(8,128)(2,1)}, u32[]{:S(2)}) copy-start(bf16[4,128,64]{2,1,0:T(8,128)(2,1)} %constant.34.clone.refs_8_) | copy-start | bytes 196612
  7.0 0.9 %copy-start.9 = (bf16[256,192]{1,0:T(8,128)(2,1)S(1)}, bf16[256,192]{1,0:T(8,128)(2,1)}, u32[]{:S(2)}) copy-start(bf16[256,192]{1,0:T(8,128)(2,1)} %constant.28.clone.refs_2_) | copy-start | bytes 294916
  7.9 0.9 %copy-start.10 = (bf16[256,144]{1,0:T(8,128)(2,1)S(1)}, bf16[256,144]{1,0:T(8,128)(2,1)}, u32[]{:S(2)}) copy-start(bf16[256,144]{1,0:T(8,128)(2,1)} %constant.26.clone.refs_0_) | copy-start | bytes 221188
  8.8 0.9 %copy-start.11 = (bf16[192,144]{1,0:T(8,128)(2,1)S(1)}, bf16[192,144]{1,0:T(8,128)(2,1)}, u32[]{:S(2)}) copy-start(bf16[192,144]{1,0:T(8,128)(2,1)} %constant.29.clone.refs_3_) | copy-start | bytes 165892
  9.7 0.9 %copy-start.12 = (bf16[160,192]{1,0:T(8,128)(2,1)S(1)}, bf16[160,192]{1,0:T(8,128)(2,1)}, u32[]{:S(2)}) copy-start(bf16[160,192]{1,0:T(8,128)(2,1)} %refs_15_.1) | copy-start | bytes 184324
  10.6 0.9 %copy-start.13 = (f32[144,1]{1,0:T(8,128)S(1)}, f32[144,1]{1,0:T(8,128)}, u32[]{:S(2)}) copy-start(f32[144,1]{1,0:T(8,128)} %constant.32.clone.refs_6_) | copy-start | bytes 1732
  11.5 0.9 %copy-start.14 = (bf16[144,256]{1,0:T(8,128)(2,1)S(1)}, bf16[144,256]{1,0:T(8,128)(2,1)}, u32[]{:S(2)}) copy-start(bf16[144,256]{1,0:T(8,128)(2,1)} %constant.27.clone.refs_1_) | copy-start | bytes 221188
  12.4 0.7 copy-start.16
  13.1 0.7 copy-start.17
  13.8 0.7 copy-start.18
  14.5 0.7 copy-start.19

commit v3 on v2

--- a/solution.py
+++ b/solution.py
@@ -122,27 +122,26 @@
 
 
 def block_forward(x, b, w, bias, saved, final):
-    gains, qkv_w, proj_w, up_w, down_w, heads = w
     unit0, scale0 = centre(x)
-    hidden = (unit0 * gains[b, 0:1, :]).astype(bf16)
-    qkv = dot(hidden, qkv_w[b]).astype(bf16)
+    hidden = (unit0 * w["gains"][b, 0:1, :]).astype(bf16)
+    qkv = dot(hidden, w["qkv"][b]).astype(bf16)
     saved["qkv"][b] = qkv
     query = qkv[:, :WIDTH]
     key = qkv[:, WIDTH : 2 * WIDTH]
     value = qkv[:, 2 * WIDTH :]
     mixed = None
     for h in range(HEADS):
-        head = heads[h]
+        head = w["heads"][h]
         score = dot(query * head.astype(bf16), key, NT) * 32 ** (-0.5) + bias[h]
         expo = jnp.exp(score - jnp.max(score, -1, keepdims=True))
         prob = expo / jnp.sum(expo, -1, keepdims=True)
         saved["prob"][b, h] = prob
         part = dot(prob.astype(bf16), value) * head
         mixed = part if mixed is None else mixed + part
-    resid = x + dot(mixed.astype(bf16), proj_w[b])
+    resid = x + dot(mixed.astype(bf16), w["proj"][b])
     unit1, scale1 = centre(resid)
-    normed = (unit1 * gains[b, 1:2, :]).astype(bf16)
-    upward = dot(normed, up_w[b])
+    normed = (unit1 * w["gains"][b, 1:2, :]).astype(bf16)
+    upward = dot(normed, w["up"][b])
     saved["unit0"][b] = unit0
     saved["scale0"][b] = scale0
     saved["unit1"][b] = unit1
@@ -151,7 +150,7 @@
     if final:
         return None
     active = 0.5 * upward * (1.0 + lax.erf(upward * 2 ** (-0.5)))
-    return resid + dot(active.astype(bf16), down_w[b])
+    return resid + dot(active.astype(bf16), w["down"][b], NT)
 
 
 def gelu_slope(b, saved):
@@ -161,19 +160,18 @@
 
 
 def block_backward(dout, b, w, saved):
-    gains, qkv_w, proj_w, up_w, down_w, heads = w
-    dactive = dot(dout.astype(bf16), down_w[b], NT).astype(bf16).astype(f32)
+    dactive = dot(dout.astype(bf16), w["down"][b]).astype(bf16).astype(f32)
     dupward = dactive * saved["slope"][...]
-    dnormed = dot(dupward.astype(bf16), up_w[b], NT).astype(bf16).astype(f32)
-    dresid = dout + norm_backward(saved["unit1"][b], saved["scale1"][b], gains[b, 1:2, :], dnormed)
-    dmixed = dot(dresid.astype(bf16), proj_w[b], NT).astype(bf16)
+    dnormed = dot(dupward.astype(bf16), w["up"][b], NT).astype(bf16).astype(f32)
+    dresid = dout + norm_backward(saved["unit1"][b], saved["scale1"][b], w["gains"][b, 1:2, :], dnormed)
+    dmixed = dot(dresid.astype(bf16), w["proj"][b], NT).astype(bf16)
     qkv = saved["qkv"][b]
     query = qkv[:, :WIDTH]
     key = qkv[:, WIDTH : 2 * WIDTH]
     value = qkv[:, 2 * WIDTH :]
     dquery = dkey = dvalue = None
     for h in range(HEADS):
-        head = heads[h]
+        head = w["heads"][h]
         narrow = head.astype(bf16)
         prob = saved["prob"][b, h]
         dmixed_h = dmixed * narrow
@@ -187,8 +185,8 @@
         dkey = dk if dkey is None else dkey + dk
         dvalue = dv if dvalue is None else dvalue + dv
     dqkv = jnp.concatenate((dquery, dkey, dvalue), 1).astype(bf16)
-    dhidden = dot(dqkv, qkv_w[b], NT).astype(bf16).astype(f32)
-    return dresid + norm_backward(saved["unit0"][b], saved["scale0"][b], gains[b, 0:1, :], dhidden)
+    dhidden = dot(dqkv, w["qkv"][b], NT).astype(bf16).astype(f32)
+    return dresid + norm_backward(saved["unit0"][b], saved["scale0"][b], w["gains"][b, 0:1, :], dhidden)
 
 
 def wait_bytes(buffer, start, count, sem):
@@ -222,20 +220,26 @@
         ).start()
 
 
+class Loads:
+    def __init__(self, names, sources, targets, sems):
+        self.targets = dict(zip(names, targets))
+        self.copies = {}
+        for i, name in enumerate(names):
+            copy = pltpu.make_async_copy(sources[i], targets[i], sems.at[i])
+            copy.start()
+            self.copies[name] = copy
+
+    def __getitem__(self, name):
+        copy = self.copies.pop(name, None)
+        if copy is not None:
+            copy.wait()
+        return self.targets[name]
+
+
 def whole_kernel(names, owners, unit, *refs):
-    consts = dict(zip(names, refs))
+    count = len(names)
+    consts = Loads(names, refs[:count], refs[-count - 1 : -1], refs[-1])
     (
-        upper_ref,
-        surface_ref,
-        upper_embed,
-        surface_embed,
-        gains,
-        qkv_w,
-        proj_w,
-        up_w,
-        down_w,
-        table_ref,
-        grad_ref,
         latent_out,
         upper_out,
         surface_out,
@@ -268,7 +272,7 @@
         last,
         result,
         sems,
-    ) = refs[len(names) :]
+    ) = refs[count : -count - 1]
     lon_count = lax.axis_size("lon")
     lat_count = lax.axis_size("lat")
     section_count = lax.axis_size("section")
@@ -308,7 +312,7 @@
     natural[...] = jnp.zeros_like(natural)
     for z in range(2):
         for a in range(6):
-            natural[z * 6 + a, 0:12, :] = grad_ref[z, a].astype(f32)
+            natural[z * 6 + a, 0:12, :] = consts["grad"][z, a].astype(f32)
     octants = dot(consts["nat_to_oct"][...], natural[...].reshape(192, WIDTH).astype(bf16))
     grad_send[...] = octants.astype(bf16).reshape(8, 32, WIDTH)
 
@@ -318,10 +322,10 @@
     for v in range(5):
         for a in range(2):
             row = (v * 2 + a) * 24
-            field[row : row + 24, :] = upper_ref[v, 2 + a].astype(f32)
-            field[256 + row : 256 + row + 24, :] = upper_ref[v, 4 * section + a].astype(f32)
+            field[row : row + 24, :] = consts["upper"][v, 2 + a].astype(f32)
+            field[256 + row : 256 + row + 24, :] = consts["upper"][v, 4 * section + a].astype(f32)
     for v in range(4):
-        field[512 + 24 * v : 512 + 24 * v + 24, :] = surface_ref[v].astype(f32)
+        field[512 + 24 * v : 512 + 24 * v + 24, :] = consts["surface"][v].astype(f32)
     fields = field[...].astype(bf16)
     same = consts["key_tok"][...] == consts["key_row"][section]
     upper_total = surface_total = None
@@ -335,14 +339,15 @@
         surface_total = surface_c if surface_total is None else surface_total + surface_c
     patch_upper[...] = upper_total.astype(bf16)
     patch_surface[...] = surface_total.astype(bf16)
-    latent = dot(patch_upper[...], upper_embed[...]) + dot(patch_surface[...], surface_embed[...])
+    latent = dot(patch_upper[...], consts["upper_embed"][...])
+    latent = latent + dot(patch_surface[...], consts["surface_embed"][...])
     latent = latent.astype(bf16).astype(f32)
-    build_bias(table_ref.at[0], consts["spread"], tab, strip, bias0)
+    build_bias(consts["table"].at[0], consts["spread"], tab, strip, bias0)
 
     pl.semaphore_wait(barrier, lon_count - 1 + group - 1 + 6)
     send_octants(grad_send, grad_recv, sems.at[0], sems.at[1], True)
 
-    w = (gains, qkv_w, proj_w, up_w, down_w, consts["heads"])
+    w = consts
     saved = {
         "qkv": qkv_s,
         "prob": prob_s,
@@ -358,7 +363,7 @@
     x_send[...] = octants.astype(bf16).reshape(8, 32, WIDTH)
     send_octants(x_send, x_recv, sems.at[2], sems.at[3], True)
 
-    build_bias(table_ref.at[1], consts["spread"], tab, strip, bias1)
+    build_bias(consts["table"].at[1], consts["spread"], tab, strip, bias1)
     last_section = (section == section_count - 1).astype(f32)
     last_band = (lat == lat_count - 1).astype(f32)
     apart = jnp.abs(consts["place_col"][0] - consts["place_row"][0]) * last_section
@@ -490,7 +495,33 @@
     out_grad,
 ):
     consts = tables()
-    names = tuple(consts)
+    operands = {
+        "upper": upper_fields,
+        "surface": surface_fields,
+        "pick": consts["pick"],
+        "key_tok": consts["key_tok"],
+        "key_row": consts["key_row"],
+        "fold_upper": consts["fold_upper"],
+        "fold_surface": consts["fold_surface"],
+        "upper_embed": upper_embed,
+        "surface_embed": surface_embed,
+        "table": earth_bias.reshape(2, HEADS, -1),
+        "spread": consts["spread"],
+        "grad": out_grad,
+        "nat_to_oct": consts["nat_to_oct"],
+        "gains": norm_gains,
+        "qkv": qkv_weight,
+        "heads": consts["heads"],
+        "proj": proj_weight,
+        "up": up_weight,
+        "down": down_weight.swapaxes(1, 2),
+        "tok_to_oct": consts["tok_to_oct"],
+        "oct_to_tok": consts["oct_to_tok"],
+        "tok_to_nat": consts["tok_to_nat"],
+        "place_col": consts["place_col"],
+        "place_row": consts["place_row"],
+    }
+    names = tuple(operands)
     lon_count = lax.axis_size("lon")
     group = lax.axis_size("lat") * lax.axis_size("section")
     unit = -(-21 // lon_count)
@@ -503,7 +534,7 @@
             jax.ShapeDtypeStruct((160, WIDTH), f32),
             jax.ShapeDtypeStruct((64, WIDTH), f32),
         ),
-        in_specs=[vmem] * (len(names) + 11),
+        in_specs=[pl.BlockSpec(memory_space=pltpu.HBM)] * len(names),
         out_specs=(vmem,) * 3,
         scratch_shapes=[
             pltpu.VMEM((FIELD_ROWS, 48), f32),
@@ -535,24 +566,13 @@
             pltpu.VMEM((unit, 16, 128), bf16),
             pltpu.VMEM((owners * unit, 16, 128), bf16),
             pltpu.SemaphoreType.DMA((12,)),
+            *(pltpu.VMEM(a.shape, a.dtype) for a in operands.values()),
+            pltpu.SemaphoreType.DMA((len(names),)),
         ],
         compiler_params=pltpu.CompilerParams(
-            collective_id=0, has_side_effects=True, vmem_limit_bytes=48 * 2**20
+            collective_id=0, has_side_effects=True, vmem_limit_bytes=int(56 * 2**20)
         ),
-    )(
-        *consts.values(),
-        upper_fields,
-        surface_fields,
-        upper_embed,
-        surface_embed,
-        norm_gains,
-        qkv_weight,
-        proj_weight,
-        up_weight,
-        down_weight,
-        earth_bias.reshape(2, HEADS, -1),
-        out_grad,
-    )
+    )(*operands.values())
 
 
 def solution(mesh):

time: 78.1 us -> 66.6 us (0.85)
  local copies, waits for them, and re-layouts: 16.4 us -> 5.51 us
    unnamed x47 -> x10, local copies, waits for them, and re-layouts: 15.6 us -> 3.16 us
    pallas_call x1, local copies, waits for them, and re-layouts: 0.71 us -> 1.64 us  [on_device(): pl.pallas_call(functools.partial(whole_kernel, names, owners, unit), out_...]
where the time goes in v3:
time: 66.6 us; the launch traced here: 66.4 us
  Pallas kernels  60.2 us (90%)
  local copies, waits for them, and re-layouts  5.51 us (8%)
    pallas_call x1, Pallas kernels, on_device(): pl.pallas_call(functools.partial(whole_kernel, names, owners, unit), out_...  60.2 us
    unnamed x10, local copies, waits for them, and re-layouts  3.16 us
    pallas_call x1, local copies, waits for them, and re-layouts, on_device(): pl.pallas_call(functools.partial(whole_kernel, names, owners, unit), out_...  1.64 us

profile of v3, /device:TPU:1, one launch (start us, length us, event | category | flops | bytes accessed | tf_op | source)
XLA Modules:
  0.0 66.4 jit_solution(12816908699713491719)
XLA Ops:
  0.6 0.0 copy-start.1
  0.6 1.6 %copy.31.refs_11_ = bf16[2,6,12,192]{3,2,1,0:T(8,128)(2,1)} copy(bf16[2,6,12,192]{3,0,2,1:T(2,128)(2,1)} %param.34) | data formatting | bytes 110592 | tf_op args[10]
  2.2 0.0 copy-done.1
  2.2 0.1 copy.34
  2.3 0.7 %copy.30.refs_9_ = f32[2,6,3312]{2,1,0:T(8,128)} copy(f32[2,6,3312]{2,0,1:T(2,128)S(1)} %bitcast.4) | data formatting | bytes 317952 | tf_op jit(solution)/shard_map/reshape | solution.py:508
  3.0 60.2 %shard_map.247 = (bf16[2,6,12,192]{3,2,1,0:T(8,128)(2,1)}, f32[160,192]{1,0:T(8,128)}, f32[64,192]{1,0:T(8,128)}) custom-call(bf16[5,6,24,48]{3,2,1,0:T(8,128)(2,1)} %refs_0_.1, bf16[4,24,48]{2,1,0:T(8,128)(2,1)} %refs_1_.1, bf16[4,144,48]{2,1,0:T(8,128)(2,1)} %constant.26.clone.refs_2_, f32[144,1]{1,0:T(8,128)} %constant.27.clone.refs_3_, ...), custom_call_target="tpu_custom_call" | custom-call | tf_op jit(solution)/shard_map/pallas_call | solution.py:530
  63.3 0.0 copy-start
  63.3 1.6 %copy.32 = bf16[2,6,12,192]{3,0,2,1:T(2,128)(2,1)} copy(bf16[2,6,12,192]{3,2,1,0:T(8,128)(2,1)} %get-tuple-element.6) | data formatting | bytes 110592 | tf_op jit(solution)/shard_map/pallas_call | solution.py:530
  64.9 0.0 copy-done
  64.9 0.0 copy-start.2
  64.9 0.7 %copy.37 = f32[160,192]{1,0:T(8,128)} copy(f32[160,192]{1,0:T(8,128)S(1)} %copy-done) | data formatting | bytes 245760
  65.6 0.2 copy-done.2
  65.8 0.6 copy.38
Async XLA Ops:
  0.6 1.6 %copy-start.1 = (f32[2,1,1,6,3312]{4,2,3,1,0:T(1,128)S(1)}, f32[2,1,1,6,3312]{4,2,3,1,0:T(1,128)}, u32[]{:S(2)}) copy-start(f32[2,1,1,6,3312]{4,2,3,1,0:T(1,128)} %param.33) | copy-start | bytes 476932
  63.3 1.7 %copy-start = (f32[160,192]{1,0:T(8,128)S(1)}, f32[160,192]{1,0:T(8,128)}, u32[]{:S(2)}) copy-start(f32[160,192]{1,0:T(8,128)} %get-tuple-element.13) | copy-start | bytes 368644
  64.9 0.9 %copy-start.2 = (f32[64,192]{1,0:T(8,128)S(1)}, f32[64,192]{1,0:T(8,128)}, u32[]{:S(2)}) copy-start(f32[64,192]{1,0:T(8,128)} %get-tuple-element.14) | copy-start | bytes 147460

commit v4 on v3

--- a/solution.py
+++ b/solution.py
@@ -29,13 +29,19 @@
     t = np.arange(TOKENS)
     col, level, row = t // 12, t // 6 % 2, t % 6
     octant = (col // 6) * 4 + level * 2 + row // 3
-    place = octant * 32 + (col % 6) * 3 + row % 3
-    tok_to_oct = np.zeros((256, TOKENS))
-    tok_to_oct[place, t] = 1
-    natural = (level * 6 + row) * 16 + col
-    nat_to_oct = np.zeros((256, 192))
-    nat_to_oct[place, natural] = 1
-    tok_to_nat = np.zeros((192, TOKENS))
+    inner = (col % 6) * 3 + row % 3
+    natural = (row * 12 + col) * 2 + level
+
+    def packing(order):
+        pack = np.zeros((256, 3, TOKENS))
+        pack[octant * 32 + inner, 0, order] = 1
+        first = inner < 9
+        pack[(octant * 32 + 18 + inner)[first], 1, order[first]] = 1
+        pack[(octant * 32 + 9 + inner)[~first], 2, order[~first]] = 1
+        return pack.reshape(256, 3 * TOKENS)
+
+    pack_tok = packing(t)
+    tok_to_nat = np.zeros((TOKENS, TOKENS))
     tok_to_nat[natural, t] = 1
     pick = np.zeros((4, TOKENS, 48))
     for c in range(4):
@@ -69,9 +75,9 @@
     place_col = np.stack((level, row // 3)).reshape(2, TOKENS, 1)
     place_row = np.stack((level, row // 3)).reshape(2, 1, TOKENS)
     return {
-        "tok_to_oct": tok_to_oct.astype(jnp.bfloat16),
-        "oct_to_tok": tok_to_oct.T.astype(jnp.bfloat16),
-        "nat_to_oct": nat_to_oct.astype(jnp.bfloat16),
+        "pack_tok": pack_tok.astype(jnp.bfloat16),
+        "unpack_tok": pack_tok.T.astype(jnp.bfloat16),
+        "pack_nat": packing(natural).astype(jnp.bfloat16),
         "tok_to_nat": tok_to_nat.astype(jnp.bfloat16),
         "pick": pick.astype(jnp.bfloat16),
         "key_row": key_row.astype(np.float32),
@@ -100,12 +106,12 @@
     return scale * (scaled - first - unit * second)
 
 
-def build_bias(table_ref, spread_ref, tab, strip, bias):
+def build_bias(table_ref, b, spread_ref, tab, strip, bias):
     for z in range(2):
         for zt in range(2):
             for a in range(6):
                 start = ((zt * 2 + z) * 6 + a) * 138
-                tab[z, (zt * 6 + a) * 8 : (zt * 6 + a) * 8 + 6, :] = table_ref[:, start : start + 138]
+                tab[z, (zt * 6 + a) * 8 : (zt * 6 + a) * 8 + 6, :] = table_ref[6 * b : 6 * b + 6, 0, start : start + 138]
     total = None
     for z in range(2):
         rest = tab[z]
@@ -189,35 +195,80 @@
     return dresid + norm_backward(saved["unit0"][b], saved["scale0"][b], w["gains"][b, 0:1, :], dhidden)
 
 
+def pack_octants(pack, tokens):
+    low, high = tokens[:, :128], tokens[:, 128:]
+    empty = jnp.zeros_like(high)
+    parts = (low, jnp.concatenate((high, empty), 1), jnp.concatenate((empty, high), 1))
+    rows = jnp.concatenate([part.astype(bf16) for part in parts], 0)
+    return dot(pack, rows).astype(bf16).reshape(8, 32, 128)
+
+
+def unpack_octants(unpack, octants):
+    parts = dot(unpack, octants.reshape(256, 128))
+    low = parts[:TOKENS]
+    left = parts[TOKENS : 2 * TOKENS]
+    right = parts[2 * TOKENS :]
+    return jnp.concatenate((low, left[:, :64] + right[:, 64:]), 1)
+
+
 def wait_bytes(buffer, start, count, sem):
     view = buffer.at[pl.ds(start, count)]
     pltpu.make_async_copy(view, view, sem).wait()
 
 
-def send_octants(src, dst, send_sem, recv_sem, forward):
-    lon_count, lat_count = lax.axis_size("lon"), lax.axis_size("lat")
-    lon, lat, section = lax.axis_index("lon"), lax.axis_index("lat"), lax.axis_index("section")
-    for k in range(8):
-        step = tuple((1 - (k >> bit & 1)) if forward else (k >> bit & 1) for bit in (2, 1, 0))
-        if step == (0, 0, 0):
-            dst[7 - k] = src[k]
-            continue
-        sign = -1 if forward else 1
+class Routes:
+    def __init__(self):
+        self.lon, self.lat, self.section = (lax.axis_index(n) for n in ("lon", "lat", "section"))
+        self.lons, self.lats, self.sections = (lax.axis_size(n) for n in ("lon", "lat", "section"))
+        self.inner = min(8, self.lons)
+        self.outer = self.lons // self.inner
+        hops = lambda d, n: min(d, n - d)
+        self.lon_steps = sorted(
+            ((a, b) for a in range(self.outer) for b in range(self.inner) if a or b),
+            key=lambda d: -(2 * (d[0] > 0) + hops(d[1], self.inner)),
+        )
+        self.group_steps = sorted(
+            ((a, b) for a in range(self.sections) for b in range(self.lats) if a or b),
+            key=lambda d: -(4 * d[0] + hops(d[1], self.lats) / 2),
+        )
+
+    def lon_peer(self, step):
+        outer = lax.rem(self.lon // self.inner + step[0], self.outer)
+        return outer * self.inner + lax.rem(self.lon + step[1], self.inner)
+
+    def group_peer(self, step):
         target = {}
         if step[0]:
-            target["lon"] = lax.rem(lon + sign + lon_count, lon_count)
+            target["section"] = lax.rem(self.section + step[0], self.sections)
         if step[1]:
-            target["section"] = 1 - section
+            target["lat"] = lax.rem(self.lat + step[1], self.lats)
+        return target
+
+    def corner(self, step, sign):
+        target = {}
+        if step[0]:
+            target["lon"] = lax.rem(self.lon + sign + self.lons, self.lons)
+        if step[1]:
+            target["section"] = 1 - self.section
         if step[2]:
-            target["lat"] = lax.rem(lat + sign + lat_count, lat_count)
+            target["lat"] = lax.rem(self.lat + sign + self.lats, self.lats)
+        return target
+
+
+def send_octants(routes, src, dst, send_sem, recv_sem, forward):
+    for far in (7, 3, 6, 2, 5, 1, 4):
+        step = (far >> 2, far >> 1 & 1, far & 1)
+        k = 7 - far if forward else far
         pltpu.make_async_remote_copy(
             src_ref=src.at[k],
             dst_ref=dst.at[7 - k],
             send_sem=send_sem,
             recv_sem=recv_sem,
-            device_id=target,
+            device_id=routes.corner(step, -1 if forward else 1),
             device_id_type=MESH,
         ).start()
+    stay = 7 if forward else 0
+    dst[7 - stay] = src[stay]
 
 
 class Loads:
@@ -244,7 +295,6 @@
         upper_out,
         surface_out,
         field,
-        natural,
         tab,
         strip,
         bias0,
@@ -271,50 +321,22 @@
         across,
         last,
         result,
+        latent_s,
+        upper_s,
+        surface_s,
         sems,
     ) = refs[count : -count - 1]
-    lon_count = lax.axis_size("lon")
-    lat_count = lax.axis_size("lat")
-    section_count = lax.axis_size("section")
-    lon = lax.axis_index("lon")
-    lat = lax.axis_index("lat")
-    section = lax.axis_index("section")
+    routes = Routes()
+    lon, lat, section = routes.lon, routes.lat, routes.section
+    lon_count, lat_count, section_count = routes.lons, routes.lats, routes.sections
     group = lat_count * section_count
     mine = section * lat_count + lat
     barrier = pltpu.get_barrier_semaphore()
-
-    def peer_of(d):
-        other = lax.rem(mine + d, group)
-        return {"lat": lax.rem(other, lat_count), "section": other // lat_count}
-
-    def greet_lon(d, carry):
-        pl.semaphore_signal(
-            barrier, inc=1, device_id={"lon": lax.rem(lon + d, lon_count)}, device_id_type=MESH
-        )
-        return carry
-
-    def greet_group(d, carry):
-        pl.semaphore_signal(barrier, inc=1, device_id=peer_of(d), device_id_type=MESH)
-        return carry
-
-    for sign in (-1, 1):
-        lon_next = lax.rem(lon + sign + lon_count, lon_count)
-        lat_next = lax.rem(lat + sign + lat_count, lat_count)
-        for target in (
-            {"lon": lon_next, "section": 1 - section},
-            {"lon": lon_next, "lat": lat_next},
-            {"lon": lon_next, "lat": lat_next, "section": 1 - section},
-        ):
-            pl.semaphore_signal(barrier, inc=1, device_id=target, device_id_type=MESH)
-    lax.fori_loop(1, lon_count, greet_lon, 0)
-    lax.fori_loop(1, group, greet_group, 0)
-
-    natural[...] = jnp.zeros_like(natural)
-    for z in range(2):
-        for a in range(6):
-            natural[z * 6 + a, 0:12, :] = consts["grad"][z, a].astype(f32)
-    octants = dot(consts["nat_to_oct"][...], natural[...].reshape(192, WIDTH).astype(bf16))
-    grad_send[...] = octants.astype(bf16).reshape(8, 32, WIDTH)
+    targets = [routes.corner(step, sign) for step in ((1, 1, 1), (1, 1, 0), (1, 0, 1)) for sign in (-1, 1)]
+    targets += [{"lon": routes.lon_peer(step)} for step in routes.lon_steps]
+    targets += [routes.group_peer(step) for step in routes.group_steps]
+    for target in targets:
+        pl.semaphore_signal(barrier, inc=1, device_id=target, device_id_type=MESH)
 
     field[240:256, :] = jnp.zeros((16, 48), f32)
     field[496:512, :] = jnp.zeros((16, 48), f32)
@@ -342,10 +364,7 @@
     latent = dot(patch_upper[...], consts["upper_embed"][...])
     latent = latent + dot(patch_surface[...], consts["surface_embed"][...])
     latent = latent.astype(bf16).astype(f32)
-    build_bias(consts["table"].at[0], consts["spread"], tab, strip, bias0)
-
-    pl.semaphore_wait(barrier, lon_count - 1 + group - 1 + 6)
-    send_octants(grad_send, grad_recv, sems.at[0], sems.at[1], True)
+    build_bias(consts["table"], 0, consts["spread"], tab, strip, bias0)
 
     w = consts
     saved = {
@@ -359,31 +378,32 @@
         "slope": slope_s,
     }
     first = block_forward(latent, 0, w, bias0, saved, False)
-    octants = dot(consts["tok_to_oct"][...], first.astype(bf16))
-    x_send[...] = octants.astype(bf16).reshape(8, 32, WIDTH)
-    send_octants(x_send, x_recv, sems.at[2], sems.at[3], True)
-
-    build_bias(consts["table"].at[1], consts["spread"], tab, strip, bias1)
+    x_send[...] = pack_octants(consts["pack_tok"][...], first)
+    pl.semaphore_wait(barrier, len(targets))
+    send_octants(routes, x_send, x_recv, sems.at[2], sems.at[3], True)
+
+    out_grad = consts["grad"][...].astype(f32).reshape(TOKENS, WIDTH)
+    grad_send[...] = pack_octants(consts["pack_nat"][...], out_grad)
+    send_octants(routes, grad_send, grad_recv, sems.at[0], sems.at[1], True)
+    build_bias(consts["table"], 1, consts["spread"], tab, strip, bias1)
     last_section = (section == section_count - 1).astype(f32)
     last_band = (lat == lat_count - 1).astype(f32)
     apart = jnp.abs(consts["place_col"][0] - consts["place_row"][0]) * last_section
     apart = apart + jnp.abs(consts["place_col"][1] - consts["place_row"][1]) * last_band
     for h in range(HEADS):
         bias1[h] = jnp.where(apart > 0.5, -1e30, bias1[h])
-    wait_bytes(grad_recv, 1, 7, sems.at[1])
-    dshifted = dot(consts["oct_to_tok"][...], grad_recv[...].reshape(256, WIDTH))
     wait_bytes(x_recv, 1, 7, sems.at[3])
-    shifted = dot(consts["oct_to_tok"][...], x_recv[...].reshape(256, WIDTH))
-
+    shifted = unpack_octants(consts["unpack_tok"][...], x_recv[...])
     block_forward(shifted, 1, w, bias1, saved, True)
     gelu_slope(1, saved)
+    wait_bytes(grad_recv, 1, 7, sems.at[1])
+    dshifted = unpack_octants(consts["unpack_tok"][...], grad_recv[...])
     dmiddle = block_backward(dshifted, 1, w, saved)
-    octants = dot(consts["tok_to_oct"][...], dmiddle.astype(bf16))
-    back_send[...] = octants.astype(bf16).reshape(8, 32, WIDTH)
-    send_octants(back_send, back_recv, sems.at[4], sems.at[5], False)
+    back_send[...] = pack_octants(consts["pack_tok"][...], dmiddle)
+    send_octants(routes, back_send, back_recv, sems.at[4], sems.at[5], False)
     gelu_slope(0, saved)
     wait_bytes(back_recv, 0, 7, sems.at[5])
-    dfirst = dot(consts["oct_to_tok"][...], back_recv[...].reshape(256, WIDTH))
+    dfirst = unpack_octants(consts["unpack_tok"][...], back_recv[...])
     dlatent = block_backward(dfirst, 0, w, saved).astype(bf16)
 
     upper_terms = dot(patch_upper[...], dlatent, TN)
@@ -394,29 +414,23 @@
     low = jnp.concatenate((low[:112], low[112:]), 1)
     terms[14:21, :, :] = low.astype(bf16).reshape(7, 16, 128)
 
-    def scatter(d, carry):
-        peer = lax.rem(lon + d, lon_count)
+    for k, step in enumerate(routes.lon_steps):
+        peer = routes.lon_peer(step)
 
         @pl.when(peer < owners)
         def _():
             pltpu.make_async_remote_copy(
                 src_ref=terms.at[pl.ds(peer * unit, unit)],
-                dst_ref=held.at[pl.ds((d - 1) * unit, unit)],
+                dst_ref=held.at[pl.ds(k * unit, unit)],
                 send_sem=sems.at[6],
                 recv_sem=sems.at[7],
                 device_id={"lon": peer},
                 device_id_type=MESH,
             ).start()
 
-        return carry
-
-    lax.fori_loop(1, lon_count, scatter, 0)
-
-    grads = dot(consts["tok_to_nat"][...], dlatent).astype(bf16)
-    for z in range(2):
-        for a in range(6):
-            k = (z * 6 + a) * 16
-            latent_out[z, a] = grads[k : k + 16][:12]
+    latent_s[...] = dot(consts["tok_to_nat"][...], dlatent).reshape(6, 12, 2, WIDTH).astype(bf16)
+    latent_copy = pltpu.make_async_copy(latent_s, latent_out, sems.at[12])
+    latent_copy.start()
 
     @pl.when(lon < owners)
     def _():
@@ -427,18 +441,16 @@
         piece[...] = total.astype(bf16)
         across[pl.ds(mine * unit, unit)] = total.astype(bf16)
 
-        def exchange(d, carry):
+        for step in routes.group_steps:
             pltpu.make_async_remote_copy(
                 src_ref=piece,
                 dst_ref=across.at[pl.ds(mine * unit, unit)],
                 send_sem=sems.at[8],
                 recv_sem=sems.at[9],
-                device_id=peer_of(d),
+                device_id=routes.group_peer(step),
                 device_id_type=MESH,
             ).start()
-            return carry
-
-        lax.fori_loop(1, group, exchange, 0)
+
         wait_bytes(across, 0, (group - 1) * unit, sems.at[9])
         whole = across[0:unit].astype(f32)
         for d in range(1, group):
@@ -446,18 +458,16 @@
         last[...] = whole.astype(bf16)
         result[pl.ds(lon * unit, unit)] = whole.astype(bf16)
 
-        def gather(d, carry):
+        for step in routes.lon_steps:
             pltpu.make_async_remote_copy(
                 src_ref=last,
                 dst_ref=result.at[pl.ds(lon * unit, unit)],
                 send_sem=sems.at[10],
                 recv_sem=sems.at[11],
-                device_id={"lon": lax.rem(lon + d, lon_count)},
+                device_id={"lon": routes.lon_peer(step)},
                 device_id_type=MESH,
             ).start()
-            return carry
-
-        lax.fori_loop(1, lon_count, gather, 0)
+
         wait_bytes(terms, 0, (owners - 1) * unit, sems.at[6])
         wait_bytes(across, 0, (group - 1) * unit, sems.at[8])
         wait_bytes(result, 0, (owners - 1) * unit, sems.at[11])
@@ -471,11 +481,18 @@
     scale = float(4 * 6 * lat_count * 12 * lon_count) ** (-0.5)
     high = result[0:14].astype(f32).reshape(224, 128) * scale
     low = result[14:21].astype(f32).reshape(112, 128) * scale
-    upper_out[:, 0:128] = high[:160]
-    surface_out[:, 0:128] = high[160:]
-    upper_out[0:112, 128:192] = low[:, :64]
-    upper_out[112:160, 128:192] = low[:48, 64:]
-    surface_out[:, 128:192] = low[48:, 64:]
+    upper_s[:, 0:128] = high[:160]
+    surface_s[:, 0:128] = high[160:]
+    upper_s[0:112, 128:192] = low[:, :64]
+    upper_s[112:160, 128:192] = low[:48, 64:]
+    surface_s[:, 128:192] = low[48:, 64:]
+    upper_copy = pltpu.make_async_copy(upper_s, upper_out, sems.at[13])
+    surface_copy = pltpu.make_async_copy(surface_s, surface_out, sems.at[14])
+    upper_copy.start()
+    surface_copy.start()
+    upper_copy.wait()
+    surface_copy.wait()
+    latent_copy.wait()
     wait_bytes(grad_send, 0, 7, sems.at[0])
     wait_bytes(x_send, 0, 7, sems.at[2])
     wait_bytes(back_send, 0, 7, sems.at[4])
@@ -505,18 +522,18 @@
         "fold_surface": consts["fold_surface"],
         "upper_embed": upper_embed,
         "surface_embed": surface_embed,
-        "table": earth_bias.reshape(2, HEADS, -1),
+        "table": earth_bias.reshape(2 * HEADS, 1, -1),
         "spread": consts["spread"],
-        "grad": out_grad,
-        "nat_to_oct": consts["nat_to_oct"],
+        "grad": out_grad.transpose(1, 2, 0, 3),
         "gains": norm_gains,
         "qkv": qkv_weight,
         "heads": consts["heads"],
         "proj": proj_weight,
         "up": up_weight,
         "down": down_weight.swapaxes(1, 2),
-        "tok_to_oct": consts["tok_to_oct"],
-        "oct_to_tok": consts["oct_to_tok"],
+        "pack_tok": consts["pack_tok"],
+        "pack_nat": consts["pack_nat"],
+        "unpack_tok": consts["unpack_tok"],
         "tok_to_nat": consts["tok_to_nat"],
         "place_col": consts["place_col"],
         "place_row": consts["place_row"],
@@ -526,19 +543,18 @@
     group = lax.axis_size("lat") * lax.axis_size("section")
     unit = -(-21 // lon_count)
     owners = -(-21 // unit)
-    vmem = pl.BlockSpec(memory_space=pltpu.VMEM)
-    return pl.pallas_call(
+    hbm = pl.BlockSpec(memory_space=pltpu.HBM)
+    latent_grad, upper_grad, surface_grad = pl.pallas_call(
         functools.partial(whole_kernel, names, owners, unit),
         out_shape=(
-            jax.ShapeDtypeStruct(out_grad.shape, bf16),
+            jax.ShapeDtypeStruct((6, 12, 2, WIDTH), bf16),
             jax.ShapeDtypeStruct((160, WIDTH), f32),
             jax.ShapeDtypeStruct((64, WIDTH), f32),
         ),
-        in_specs=[pl.BlockSpec(memory_space=pltpu.HBM)] * len(names),
-        out_specs=(vmem,) * 3,
+        in_specs=[hbm] * len(names),
+        out_specs=(hbm,) * 3,
         scratch_shapes=[
             pltpu.VMEM((FIELD_ROWS, 48), f32),
-            pltpu.VMEM((12, 16, WIDTH), f32),
             pltpu.VMEM((2, 96, 138), f32),
             pltpu.VMEM((96, 276), f32),
             pltpu.VMEM((HEADS, TOKENS, TOKENS), f32),
@@ -553,19 +569,22 @@
             pltpu.VMEM((TOKENS, 768), f32),
             pltpu.VMEM((TOKENS, 160), bf16),
             pltpu.VMEM((TOKENS, 64), bf16),
-            pltpu.VMEM((8, 32, WIDTH), bf16),
-            pltpu.VMEM((8, 32, WIDTH), bf16),
-            pltpu.VMEM((8, 32, WIDTH), bf16),
-            pltpu.VMEM((8, 32, WIDTH), bf16),
-            pltpu.VMEM((8, 32, WIDTH), bf16),
-            pltpu.VMEM((8, 32, WIDTH), bf16),
+            pltpu.VMEM((8, 32, 128), bf16),
+            pltpu.VMEM((8, 32, 128), bf16),
+            pltpu.VMEM((8, 32, 128), bf16),
+            pltpu.VMEM((8, 32, 128), bf16),
+            pltpu.VMEM((8, 32, 128), bf16),
+            pltpu.VMEM((8, 32, 128), bf16),
             pltpu.VMEM((owners * unit, 16, 128), bf16),
             pltpu.VMEM(((lon_count - 1) * unit, 16, 128), bf16),
             pltpu.VMEM((unit, 16, 128), bf16),
             pltpu.VMEM((group * unit, 16, 128), bf16),
             pltpu.VMEM((unit, 16, 128), bf16),
             pltpu.VMEM((owners * unit, 16, 128), bf16),
-            pltpu.SemaphoreType.DMA((12,)),
+            pltpu.VMEM((6, 12, 2, WIDTH), bf16),
+            pltpu.VMEM((160, WIDTH), f32),
+            pltpu.VMEM((64, WIDTH), f32),
+            pltpu.SemaphoreType.DMA((15,)),
             *(pltpu.VMEM(a.shape, a.dtype) for a in operands.values()),
             pltpu.SemaphoreType.DMA((len(names),)),
         ],
@@ -573,6 +592,7 @@
             collective_id=0, has_side_effects=True, vmem_limit_bytes=int(56 * 2**20)
         ),
     )(*operands.values())
+    return latent_grad.transpose(2, 0, 1, 3), upper_grad, surface_grad
 
 
 def solution(mesh):

time: 66.6 us -> 61.5 us (0.923)
  Pallas kernels: 60.2 us -> 56.8 us
  local copies, waits for them, and re-layouts: 5.51 us -> 3.83 us
    pallas_call x1, Pallas kernels: 60.2 us -> 56.8 us  [on_device(): pl.pallas_call(functools.partial(whole_kernel, names, owners, unit), out_...]
    pallas_call x1 -> x0, local copies, waits for them, and re-layouts: 1.64 us -> none  [on_device(): pl.pallas_call(functools.partial(whole_kernel, names, owners, unit), out_...]
    reshape x1 -> x0, local copies, waits for them, and re-layouts: 0.71 us -> none  [on_device(): earth_bias.reshape(2, HEADS, -1)]
    unnamed x10 -> x5, local copies, waits for them, and re-layouts: 3.16 us -> 3.83 us
where the time goes in v4:
time: 61.5 us; the launch traced here: 61.3 us
  Pallas kernels  56.8 us (92%)
  local copies, waits for them, and re-layouts  3.83 us (6%)
  between operations  0.64 us (1%)
    pallas_call x1, Pallas kernels, on_device(): pl.pallas_call(functools.partial(whole_kernel, names, owners, unit), out_...  56.8 us
    unnamed x5, local copies, waits for them, and re-layouts  3.83 us

profile of v4, /device:TPU:1, one launch (start us, length us, event | category | flops | bytes accessed | tf_op | source)
XLA Modules:
  0.0 61.3 jit_solution(13457623683333182056)
XLA Ops:
  0.6 56.8 %shard_map.247 = (bf16[6,12,2,192]{3,2,1,0:T(2,128)(2,1)}, f32[160,192]{1,0:T(8,128)}, f32[64,192]{1,0:T(8,128)}) custom-call(bf16[5,6,24,48]{3,2,1,0:T(8,128)(2,1)} %refs_0_.1, bf16[4,24,48]{2,1,0:T(8,128)(2,1)} %refs_1_.1, bf16[4,144,48]{2,1,0:T(8,128)(2,1)} %constant.26.clone.refs_2_, f32[144,1]{1,0:T(8,128)} %constant.27.clone.refs_3_, ...), custom_call_target="tpu_custom_call" | custom-call | tf_op jit(solution)/shard_map/pallas_call | solution.py:547
  57.5 1.6 %copy.30 = bf16[2,6,12,192]{3,0,2,1:T(2,128)(2,1)} copy(bf16[2,6,12,192]{3,0,2,1:T(2,128)(2,1)} %bitcast.6) | data formatting | bytes 110592
  59.0 0.0 copy-start
  59.0 1.6 %copy.31 = f32[160,192]{1,0:T(8,128)} copy(f32[160,192]{1,0:T(8,128)} %get-tuple-element.13) | data formatting | bytes 245760
  60.7 0.0 copy-done
  60.7 0.6 %copy.32 = f32[64,192]{1,0:T(8,128)} copy(f32[64,192]{1,0:T(8,128)S(1)} %copy-done) | data formatting | bytes 98304
Async XLA Ops:
  59.0 1.6 %copy-start = (f32[64,192]{1,0:T(8,128)S(1)}, f32[64,192]{1,0:T(8,128)}, u32[]{:S(2)}) copy-start(f32[64,192]{1,0:T(8,128)} %get-tuple-element.14) | copy-start | bytes 147460

commit v5 on v4

--- a/solution.py
+++ b/solution.py
@@ -1,4 +1,5 @@
 import functools
+import itertools
 
 import jax
 import jax.numpy as jnp
@@ -222,26 +223,48 @@
         self.lons, self.lats, self.sections = (lax.axis_size(n) for n in ("lon", "lat", "section"))
         self.inner = min(8, self.lons)
         self.outer = self.lons // self.inner
+        self.pair_in, self.pair_out = min(2, self.inner), min(2, self.outer)
+        self.high = self.lon // self.inner
+        self.low = lax.rem(self.lon, self.inner)
         hops = lambda d, n: min(d, n - d)
-        self.lon_steps = sorted(
-            ((a, b) for a in range(self.outer) for b in range(self.inner) if a or b),
-            key=lambda d: -(2 * (d[0] > 0) + hops(d[1], self.inner)),
+        near = itertools.product(range(self.pair_out), range(self.pair_in), range(self.lats))
+        self.near_steps = sorted(
+            (d for d in near if any(d)), key=lambda d: -(d[0] + d[1] + hops(d[2], self.lats) / 2)
         )
-        self.group_steps = sorted(
-            ((a, b) for a in range(self.sections) for b in range(self.lats) if a or b),
-            key=lambda d: -(4 * d[0] + hops(d[1], self.lats) / 2),
+        far = itertools.product(
+            range(self.sections), range(self.outer // self.pair_out), range(self.inner // self.pair_in)
         )
-
-    def lon_peer(self, step):
-        outer = lax.rem(self.lon // self.inner + step[0], self.outer)
-        return outer * self.inner + lax.rem(self.lon + step[1], self.inner)
-
-    def group_peer(self, step):
+        self.far_steps = sorted(
+            (d for d in far if any(d)),
+            key=lambda d: -((4 - 2 * d[1] if d[0] else 2 * d[1]) + 2 * hops(d[2], self.inner // self.pair_in)),
+        )
+
+    def near_index(self, step=(0, 0, 0)):
+        out = lax.rem(self.high + step[0], self.pair_out)
+        into = lax.rem(self.low + step[1], self.pair_in)
+        return (out * self.pair_in + into) * self.lats + lax.rem(self.lat + step[2], self.lats)
+
+    def near_peer(self, step):
+        target = {}
+        if step[0] or step[1]:
+            out = self.high // self.pair_out * self.pair_out + lax.rem(self.high + step[0], self.pair_out)
+            into = self.low // self.pair_in * self.pair_in + lax.rem(self.low + step[1], self.pair_in)
+            target["lon"] = out * self.inner + into
+        if step[2]:
+            target["lat"] = lax.rem(self.lat + step[2], self.lats)
+        return target
+
+    def far_index(self):
+        index = self.section * (self.outer // self.pair_out) + self.high // self.pair_out
+        return index * (self.inner // self.pair_in) + self.low // self.pair_in
+
+    def far_peer(self, step):
         target = {}
         if step[0]:
             target["section"] = lax.rem(self.section + step[0], self.sections)
-        if step[1]:
-            target["lat"] = lax.rem(self.lat + step[1], self.lats)
+        if step[1] or step[2]:
+            out = lax.rem(self.high + step[1] * self.pair_out, self.outer)
+            target["lon"] = out * self.inner + lax.rem(self.low + step[2] * self.pair_in, self.inner)
         return target
 
     def corner(self, step, sign):
@@ -329,12 +352,13 @@
     routes = Routes()
     lon, lat, section = routes.lon, routes.lat, routes.section
     lon_count, lat_count, section_count = routes.lons, routes.lats, routes.sections
-    group = lat_count * section_count
-    mine = section * lat_count + lat
+    count_near, count_far = len(routes.near_steps), len(routes.far_steps)
+    owner, mine = routes.near_index(), routes.far_index()
     barrier = pltpu.get_barrier_semaphore()
-    targets = [routes.corner(step, sign) for step in ((1, 1, 1), (1, 1, 0), (1, 0, 1)) for sign in (-1, 1)]
-    targets += [{"lon": routes.lon_peer(step)} for step in routes.lon_steps]
-    targets += [routes.group_peer(step) for step in routes.group_steps]
+    corners = sorted(itertools.product(range(2), repeat=3), reverse=True)
+    targets = [routes.corner(d, sign) for d in corners[:-1] for sign in (-1, 1) if d != (0, 1, 0) or sign > 0]
+    targets += [routes.far_peer(step) for step in routes.far_steps]
+    targets += [routes.near_peer(step) for step in routes.near_steps]
     for target in targets:
         pl.semaphore_signal(barrier, inc=1, device_id=target, device_id_type=MESH)
 
@@ -414,8 +438,8 @@
     low = jnp.concatenate((low[:112], low[112:]), 1)
     terms[14:21, :, :] = low.astype(bf16).reshape(7, 16, 128)
 
-    for k, step in enumerate(routes.lon_steps):
-        peer = routes.lon_peer(step)
+    for k, step in enumerate(routes.near_steps):
+        peer = routes.near_index(step)
 
         @pl.when(peer < owners)
         def _():
@@ -424,7 +448,7 @@
                 dst_ref=held.at[pl.ds(k * unit, unit)],
                 send_sem=sems.at[6],
                 recv_sem=sems.at[7],
-                device_id={"lon": peer},
+                device_id=routes.near_peer(step),
                 device_id_type=MESH,
             ).start()
 
@@ -432,48 +456,46 @@
     latent_copy = pltpu.make_async_copy(latent_s, latent_out, sems.at[12])
     latent_copy.start()
 
-    @pl.when(lon < owners)
+    @pl.when(owner < owners)
     def _():
-        wait_bytes(held, 0, (lon_count - 1) * unit, sems.at[7])
-        total = terms[pl.ds(lon * unit, unit)].astype(f32)
-        for d in range(lon_count - 1):
+        wait_bytes(held, 0, count_near * unit, sems.at[7])
+        total = terms[pl.ds(owner * unit, unit)].astype(f32)
+        for d in range(count_near):
             total = total + held[d * unit : d * unit + unit].astype(f32)
         piece[...] = total.astype(bf16)
         across[pl.ds(mine * unit, unit)] = total.astype(bf16)
-
-        for step in routes.group_steps:
+        for step in routes.far_steps:
             pltpu.make_async_remote_copy(
                 src_ref=piece,
                 dst_ref=across.at[pl.ds(mine * unit, unit)],
                 send_sem=sems.at[8],
                 recv_sem=sems.at[9],
-                device_id=routes.group_peer(step),
+                device_id=routes.far_peer(step),
                 device_id_type=MESH,
             ).start()
 
-        wait_bytes(across, 0, (group - 1) * unit, sems.at[9])
+        wait_bytes(across, 0, count_far * unit, sems.at[9])
         whole = across[0:unit].astype(f32)
-        for d in range(1, group):
+        for d in range(1, count_far + 1):
             whole = whole + across[d * unit : d * unit + unit].astype(f32)
         last[...] = whole.astype(bf16)
-        result[pl.ds(lon * unit, unit)] = whole.astype(bf16)
-
-        for step in routes.lon_steps:
+        result[pl.ds(owner * unit, unit)] = whole.astype(bf16)
+        for step in routes.near_steps:
             pltpu.make_async_remote_copy(
                 src_ref=last,
-                dst_ref=result.at[pl.ds(lon * unit, unit)],
+                dst_ref=result.at[pl.ds(owner * unit, unit)],
                 send_sem=sems.at[10],
                 recv_sem=sems.at[11],
-                device_id={"lon": routes.lon_peer(step)},
+                device_id=routes.near_peer(step),
                 device_id_type=MESH,
             ).start()
 
         wait_bytes(terms, 0, (owners - 1) * unit, sems.at[6])
-        wait_bytes(across, 0, (group - 1) * unit, sems.at[8])
+        wait_bytes(across, 0, count_far * unit, sems.at[8])
         wait_bytes(result, 0, (owners - 1) * unit, sems.at[11])
-        wait_bytes(held, 0, (lon_count - 1) * unit, sems.at[10])
-
-    @pl.when(lon >= owners)
+        wait_bytes(held, 0, count_near * unit, sems.at[10])
+
+    @pl.when(owner >= owners)
     def _():
         wait_bytes(terms, 0, owners * unit, sems.at[6])
         wait_bytes(result, 0, owners * unit, sems.at[11])
@@ -496,6 +518,14 @@
     wait_bytes(grad_send, 0, 7, sems.at[0])
     wait_bytes(x_send, 0, 7, sems.at[2])
     wait_bytes(back_send, 0, 7, sems.at[4])
+
+
+def hand_over(*refs):
+    copies = [pltpu.make_async_copy(refs[k], refs[3 + k], refs[6].at[k]) for k in range(3)]
+    for copy in copies:
+        copy.start()
+    for copy in copies:
+        copy.wait()
 
 
 def on_device(
@@ -540,8 +570,11 @@
     }
     names = tuple(operands)
     lon_count = lax.axis_size("lon")
-    group = lax.axis_size("lat") * lax.axis_size("section")
-    unit = -(-21 // lon_count)
+    near = min(4, lon_count) * lax.axis_size("lat")
+    if lon_count < 16:
+        near = min(2, lon_count) * lax.axis_size("lat")
+    group = lon_count * lax.axis_size("lat") * lax.axis_size("section") // near
+    unit = -(-21 // near)
     owners = -(-21 // unit)
     hbm = pl.BlockSpec(memory_space=pltpu.HBM)
     latent_grad, upper_grad, surface_grad = pl.pallas_call(
@@ -576,7 +609,7 @@
             pltpu.VMEM((8, 32, 128), bf16),
             pltpu.VMEM((8, 32, 128), bf16),
             pltpu.VMEM((owners * unit, 16, 128), bf16),
-            pltpu.VMEM(((lon_count - 1) * unit, 16, 128), bf16),
+            pltpu.VMEM(((near - 1) * unit, 16, 128), bf16),
             pltpu.VMEM((unit, 16, 128), bf16),
             pltpu.VMEM((group * unit, 16, 128), bf16),
             pltpu.VMEM((unit, 16, 128), bf16),
@@ -592,6 +625,15 @@
             collective_id=0, has_side_effects=True, vmem_limit_bytes=int(56 * 2**20)
         ),
     )(*operands.values())
+    latent_grad, upper_grad, surface_grad = pl.pallas_call(
+        hand_over,
+        out_shape=tuple(
+            jax.ShapeDtypeStruct(a.shape, a.dtype) for a in (latent_grad, upper_grad, surface_grad)
+        ),
+        in_specs=[hbm] * 3,
+        out_specs=(hbm,) * 3,
+        scratch_shapes=[pltpu.SemaphoreType.DMA((3,))],
+    )(latent_grad, upper_grad, surface_grad)
     return latent_grad.transpose(2, 0, 1, 3), upper_grad, surface_grad
 
 

time: 61.5 us -> 66 us (1.073)
  Pallas kernels: 56.8 us -> 65.2 us
  local copies, waits for them, and re-layouts: 3.83 us -> 0 us
    pallas_call x0 -> x1, Pallas kernels: none -> 10.3 us  [on_device(): pl.pallas_call(hand_over, out_shape=tuple((jax.ShapeDtypeStruct(a.shape,...]
    unnamed x5 -> x0, local copies, waits for them, and re-layouts: 3.83 us -> none
    pallas_call x1, Pallas kernels: 56.8 us -> 54.9 us  [on_device(): pl.pallas_call(functools.partial(whole_kernel, names, owners, unit), out_...]
where the time goes in v5:
time: 66 us; the launch traced here: 65.9 us
  Pallas kernels  65.2 us (99%)
    pallas_call x1, Pallas kernels, on_device(): pl.pallas_call(functools.partial(whole_kernel, names, owners, unit), out_...  54.9 us
    pallas_call x1, Pallas kernels, on_device(): pl.pallas_call(hand_over, out_shape=tuple((jax.ShapeDtypeStruct(a.shape,...  10.3 us

profile of v5, /device:TPU:1, one launch (start us, length us, event | category | flops | bytes accessed | tf_op | source)
XLA Modules:
  0.0 65.9 jit_solution(13425007390194735976)
XLA Ops:
  0.6 54.9 %shard_map.247 = (bf16[6,12,2,192]{3,2,1,0:T(2,128)(2,1)}, f32[160,192]{1,0:T(8,128)}, f32[64,192]{1,0:T(8,128)}) custom-call(bf16[5,6,24,48]{3,2,1,0:T(8,128)(2,1)} %refs_0_.1, bf16[4,24,48]{2,1,0:T(8,128)(2,1)} %refs_1_.1, bf16[4,144,48]{2,1,0:T(8,128)(2,1)} %constant.26.clone.refs_2_, f32[144,1]{1,0:T(8,128)} %constant.27.clone.refs_3_, ...), custom_call_target="tpu_custom_call" | custom-call | tf_op jit(solution)/shard_map/pallas_call | solution.py:580
  55.5 10.3 %shard_map.248 = (bf16[6,12,2,192]{3,2,1,0:T(2,128)(2,1)}, f32[160,192]{1,0:T(8,128)}, f32[64,192]{1,0:T(8,128)}) custom-call(bf16[6,12,2,192]{3,2,1,0:T(2,128)(2,1)} %get-tuple-element.9.refs_0_, f32[160,192]{1,0:T(8,128)} %get-tuple-element.10.refs_1_, f32[64,192]{1,0:T(8,128)} %get-tuple-element.11.refs_2_), custom_call_target="tpu_custom_call" | custom-call | tf_op jit(solution)/shard_map/pallas_call | solution.py:628

commit v6 on v5

--- a/solution.py
+++ b/solution.py
@@ -14,6 +14,7 @@
 bf16 = jnp.bfloat16
 norm_eps = 1e-05
 HEADS = 6
+BATCH = 3
 TOKENS = 144
 WIDTH = 192
 FIELD_ROWS = 640
@@ -125,7 +126,18 @@
     for h in range(HEADS):
         lines = jnp.concatenate([strip[8 * k + h : 8 * k + h + 1, :] for k in range(12)], 0)
         for o in range(12):
-            bias[h, 12 * o : 12 * o + 12, :] = lines[:, 12 * (11 - o) : 12 * (11 - o) + TOKENS]
+            bias[h * TOKENS + 12 * o : h * TOKENS + 12 * o + 12, :] = lines[:, 12 * (11 - o) : 12 * (11 - o) + TOKENS]
+
+
+def by_head(values, w, first):
+    return jnp.concatenate([values * w["heads"][h].astype(bf16) for h in range(first, first + BATCH)], 0)
+
+
+def own_heads(stacked, w, first, total):
+    for k in range(BATCH):
+        part = stacked[k * TOKENS : (k + 1) * TOKENS] * w["heads"][first + k]
+        total = part if total is None else total + part
+    return total
 
 
 def block_forward(x, b, w, bias, saved, final):
@@ -137,14 +149,13 @@
     key = qkv[:, WIDTH : 2 * WIDTH]
     value = qkv[:, 2 * WIDTH :]
     mixed = None
-    for h in range(HEADS):
-        head = w["heads"][h]
-        score = dot(query * head.astype(bf16), key, NT) * 32 ** (-0.5) + bias[h]
+    for g in range(0, HEADS, BATCH):
+        rows = slice(g * TOKENS, (g + BATCH) * TOKENS)
+        score = dot(by_head(query, w, g), key, NT) * 32 ** (-0.5) + bias[rows]
         expo = jnp.exp(score - jnp.max(score, -1, keepdims=True))
-        prob = expo / jnp.sum(expo, -1, keepdims=True)
-        saved["prob"][b, h] = prob
-        part = dot(prob.astype(bf16), value) * head
-        mixed = part if mixed is None else mixed + part
+        prob = expo * (1.0 / jnp.sum(expo, -1, keepdims=True))
+        saved["prob"][b, rows] = prob
+        mixed = own_heads(dot(prob.astype(bf16), value), w, g, mixed)
     resid = x + dot(mixed.astype(bf16), w["proj"][b])
     unit1, scale1 = centre(resid)
     normed = (unit1 * w["gains"][b, 1:2, :]).astype(bf16)
@@ -177,20 +188,20 @@
     key = qkv[:, WIDTH : 2 * WIDTH]
     value = qkv[:, 2 * WIDTH :]
     dquery = dkey = dvalue = None
-    for h in range(HEADS):
-        head = w["heads"][h]
-        narrow = head.astype(bf16)
-        prob = saved["prob"][b, h]
-        dmixed_h = dmixed * narrow
-        dweights = dot(dmixed_h, value, NT).astype(bf16).astype(f32)
-        dv = dot(prob.astype(bf16), dmixed_h, TN)
+    for g in range(0, HEADS, BATCH):
+        rows = slice(g * TOKENS, (g + BATCH) * TOKENS)
+        prob = saved["prob"][b, rows]
+        dmixed_g = by_head(dmixed, w, g)
+        dweights = dot(dmixed_g, value, NT).astype(bf16).astype(f32)
+        dv = dot(prob.astype(bf16), dmixed_g, TN)
         inner = jnp.sum(dweights * prob, -1, keepdims=True)
-        dscore = (prob * (dweights - inner) * 32 ** (-0.5)).astype(bf16)
-        dq = dot(dscore, key) * head
-        dk = dot(dscore, query * narrow, TN)
-        dquery = dq if dquery is None else dquery + dq
+        dscore = (prob * (dweights - inner)).astype(bf16)
+        dquery = own_heads(dot(dscore, key), w, g, dquery)
+        dk = dot(dscore, by_head(query, w, g), TN)
         dkey = dk if dkey is None else dkey + dk
         dvalue = dv if dvalue is None else dvalue + dv
+    dquery = dquery * 32 ** (-0.5)
+    dkey = dkey * 32 ** (-0.5)
     dqkv = jnp.concatenate((dquery, dkey, dvalue), 1).astype(bf16)
     dhidden = dot(dqkv, w["qkv"][b], NT).astype(bf16).astype(f32)
     return dresid + norm_backward(saved["unit0"][b], saved["scale0"][b], w["gains"][b, 0:1, :], dhidden)
@@ -344,9 +355,6 @@
         across,
         last,
         result,
-        latent_s,
-        upper_s,
-        surface_s,
         sems,
     ) = refs[count : -count - 1]
     routes = Routes()
@@ -415,7 +423,8 @@
     apart = jnp.abs(consts["place_col"][0] - consts["place_row"][0]) * last_section
     apart = apart + jnp.abs(consts["place_col"][1] - consts["place_row"][1]) * last_band
     for h in range(HEADS):
-        bias1[h] = jnp.where(apart > 0.5, -1e30, bias1[h])
+        rows = slice(h * TOKENS, (h + 1) * TOKENS)
+        bias1[rows] = jnp.where(apart > 0.5, -1e30, bias1[rows])
     wait_bytes(x_recv, 1, 7, sems.at[3])
     shifted = unpack_octants(consts["unpack_tok"][...], x_recv[...])
     block_forward(shifted, 1, w, bias1, saved, True)
@@ -452,9 +461,7 @@
                 device_id_type=MESH,
             ).start()
 
-    latent_s[...] = dot(consts["tok_to_nat"][...], dlatent).reshape(6, 12, 2, WIDTH).astype(bf16)
-    latent_copy = pltpu.make_async_copy(latent_s, latent_out, sems.at[12])
-    latent_copy.start()
+    latent_out[...] = dot(consts["tok_to_nat"][...], dlatent).reshape(6, 12, 2, WIDTH).astype(bf16)
 
     @pl.when(owner < owners)
     def _():
@@ -503,29 +510,14 @@
     scale = float(4 * 6 * lat_count * 12 * lon_count) ** (-0.5)
     high = result[0:14].astype(f32).reshape(224, 128) * scale
     low = result[14:21].astype(f32).reshape(112, 128) * scale
-    upper_s[:, 0:128] = high[:160]
-    surface_s[:, 0:128] = high[160:]
-    upper_s[0:112, 128:192] = low[:, :64]
-    upper_s[112:160, 128:192] = low[:48, 64:]
-    surface_s[:, 128:192] = low[48:, 64:]
-    upper_copy = pltpu.make_async_copy(upper_s, upper_out, sems.at[13])
-    surface_copy = pltpu.make_async_copy(surface_s, surface_out, sems.at[14])
-    upper_copy.start()
-    surface_copy.start()
-    upper_copy.wait()
-    surface_copy.wait()
-    latent_copy.wait()
+    upper_out[:, 0:128] = high[:160]
+    surface_out[:, 0:128] = high[160:]
+    upper_out[0:112, 128:192] = low[:, :64]
+    upper_out[112:160, 128:192] = low[:48, 64:]
+    surface_out[:, 128:192] = low[48:, 64:]
     wait_bytes(grad_send, 0, 7, sems.at[0])
     wait_bytes(x_send, 0, 7, sems.at[2])
     wait_bytes(back_send, 0, 7, sems.at[4])
-
-
-def hand_over(*refs):
-    copies = [pltpu.make_async_copy(refs[k], refs[3 + k], refs[6].at[k]) for k in range(3)]
-    for copy in copies:
-        copy.start()
-    for copy in copies:
-        copy.wait()
 
 
 def on_device(
@@ -585,15 +577,15 @@
             jax.ShapeDtypeStruct((64, WIDTH), f32),
         ),
         in_specs=[hbm] * len(names),
-        out_specs=(hbm,) * 3,
+        out_specs=(pl.BlockSpec(memory_space=pltpu.VMEM),) * 3,
         scratch_shapes=[
             pltpu.VMEM((FIELD_ROWS, 48), f32),
             pltpu.VMEM((2, 96, 138), f32),
             pltpu.VMEM((96, 276), f32),
-            pltpu.VMEM((HEADS, TOKENS, TOKENS), f32),
-            pltpu.VMEM((HEADS, TOKENS, TOKENS), f32),
+            pltpu.VMEM((HEADS * TOKENS, TOKENS), f32),
+            pltpu.VMEM((HEADS * TOKENS, TOKENS), f32),
             pltpu.VMEM((2, TOKENS, 3 * WIDTH), bf16),
-            pltpu.VMEM((2, HEADS, TOKENS, TOKENS), f32),
+            pltpu.VMEM((2, HEADS * TOKENS, TOKENS), f32),
             pltpu.VMEM((2, TOKENS, WIDTH), f32),
             pltpu.VMEM((2, TOKENS, 1), f32),
             pltpu.VMEM((2, TOKENS, WIDTH), f32),
@@ -614,26 +606,14 @@
             pltpu.VMEM((group * unit, 16, 128), bf16),
             pltpu.VMEM((unit, 16, 128), bf16),
             pltpu.VMEM((owners * unit, 16, 128), bf16),
-            pltpu.VMEM((6, 12, 2, WIDTH), bf16),
-            pltpu.VMEM((160, WIDTH), f32),
-            pltpu.VMEM((64, WIDTH), f32),
-            pltpu.SemaphoreType.DMA((15,)),
+            pltpu.SemaphoreType.DMA((12,)),
             *(pltpu.VMEM(a.shape, a.dtype) for a in operands.values()),
             pltpu.SemaphoreType.DMA((len(names),)),
         ],
         compiler_params=pltpu.CompilerParams(
-            collective_id=0, has_side_effects=True, vmem_limit_bytes=int(56 * 2**20)
+            collective_id=0, has_side_effects=True, vmem_limit_bytes=40 * 2**20
         ),
-    )(*operands.values())
-    latent_grad, upper_grad, surface_grad = pl.pallas_call(
-        hand_over,
-        out_shape=tuple(
-            jax.ShapeDtypeStruct(a.shape, a.dtype) for a in (latent_grad, upper_grad, surface_grad)
-        ),
-        in_specs=[hbm] * 3,
-        out_specs=(hbm,) * 3,
-        scratch_shapes=[pltpu.SemaphoreType.DMA((3,))],
-    )(latent_grad, upper_grad, surface_grad)
+    )(*(pltpu.with_memory_space_constraint(a, pltpu.HBM) for a in operands.values()))
     return latent_grad.transpose(2, 0, 1, 3), upper_grad, surface_grad
 
 

time: 66 us -> 54.6 us (0.83)
  Pallas kernels: 65.2 us -> 51.9 us
  local copies, waits for them, and re-layouts: 0 us -> 1.93 us
    pallas_call x1 -> x0, Pallas kernels: 10.3 us -> none  [on_device(): pl.pallas_call(hand_over, out_shape=tuple((jax.ShapeDtypeStruct(a.shape,...]
    pallas_call x1, Pallas kernels: 54.9 us -> 51.9 us  [on_device(): pl.pallas_call(functools.partial(whole_kernel, names, owners, unit), out_...]
    unnamed x0 -> x3, local copies, waits for them, and re-layouts: none -> 1.93 us
where the time goes in v6:
time: 54.6 us; the launch traced here: 54.5 us
  Pallas kernels  51.9 us (95%)
  local copies, waits for them, and re-layouts  1.93 us (4%)
  between operations  0.64 us (1%)
    pallas_call x1, Pallas kernels, on_device(): pl.pallas_call(functools.partial(whole_kernel, names, owners, unit), out_...  51.9 us
    unnamed x3, local copies, waits for them, and re-layouts  1.93 us

profile of v6, /device:TPU:1, one launch (start us, length us, event | category | flops | bytes accessed | tf_op | source)
XLA Modules:
  0.0 54.5 jit_solution(6295216435547971393)
XLA Ops:
  0.6 51.9 %shard_map.247 = (bf16[6,12,2,192]{3,2,1,0:T(2,128)(2,1)S(1)}, f32[160,192]{1,0:T(8,128)S(1)}, f32[64,192]{1,0:T(8,128)S(1)}) custom-call(bf16[5,6,24,48]{3,2,1,0:T(8,128)(2,1)} %refs_0_.1, bf16[4,24,48]{2,1,0:T(8,128)(2,1)} %refs_1_.1, bf16[4,144,48]{2,1,0:T(8,128)(2,1)} %constant.26.clone.refs_2_, f32[144,1]{1,0:T(8,128)} %constant.27.clone.refs_3_, ...), custom_call_target="tpu_custom_call" | custom-call | tf_op jit(solution)/shard_map/pallas_call | solution.py:572
  52.5 0.6 %copy.30 = bf16[2,6,12,192]{3,0,2,1:T(2,128)(2,1)} copy(bf16[2,6,12,192]{3,0,2,1:T(2,128)(2,1)S(1)} %bitcast.4) | data formatting | bytes 110592
  53.2 0.7 %copy.31 = f32[160,192]{1,0:T(8,128)} copy(f32[160,192]{1,0:T(8,128)S(1)} %get-tuple-element.13) | data formatting | bytes 245760
  53.8 0.6 %copy.32 = f32[64,192]{1,0:T(8,128)} copy(f32[64,192]{1,0:T(8,128)S(1)} %get-tuple-element.14) | data formatting | bytes 98304

commit v7 on v6

--- a/solution.py
+++ b/solution.py
@@ -518,6 +518,14 @@
     wait_bytes(grad_send, 0, 7, sems.at[0])
     wait_bytes(x_send, 0, 7, sems.at[2])
     wait_bytes(back_send, 0, 7, sems.at[4])
+
+
+def hand_over(*refs):
+    copies = [pltpu.make_async_copy(refs[k], refs[3 + k], refs[6].at[k]) for k in range(3)]
+    for copy in copies:
+        copy.start()
+    for copy in copies:
+        copy.wait()
 
 
 def on_device(
@@ -614,6 +622,16 @@
             collective_id=0, has_side_effects=True, vmem_limit_bytes=40 * 2**20
         ),
     )(*(pltpu.with_memory_space_constraint(a, pltpu.HBM) for a in operands.values()))
+    latent_grad, upper_grad, surface_grad = pl.pallas_call(
+        hand_over,
+        out_shape=tuple(
+            jax.ShapeDtypeStruct(a.shape, a.dtype) for a in (latent_grad, upper_grad, surface_grad)
+        ),
+        in_specs=[pl.BlockSpec(memory_space=pltpu.VMEM)] * 3,
+        out_specs=(hbm,) * 3,
+        scratch_shapes=[pltpu.SemaphoreType.DMA((3,))],
+        compiler_params=pltpu.CompilerParams(vmem_limit_bytes=2**20),
+    )(latent_grad, upper_grad, surface_grad)
     return latent_grad.transpose(2, 0, 1, 3), upper_grad, surface_grad
 
 

time: 54.6 us -> 53.4 us (0.978)
  local copies, waits for them, and re-layouts: 1.93 us -> 0 us
  Pallas kernels: 51.9 us -> 52.6 us
    unnamed x3 -> x0, local copies, waits for them, and re-layouts: 1.93 us -> none
    pallas_call x0 -> x1, Pallas kernels: none -> 0.74 us  [on_device(): pl.pallas_call(hand_over, out_shape=tuple((jax.ShapeDtypeStruct(a.shape,...]
where the time goes in v7:
time: 53.4 us; the launch traced here: 53.3 us
  Pallas kernels  52.6 us (99%)
  between operations  0.64 us (1%)
    pallas_call x1, Pallas kernels, on_device(): pl.pallas_call(functools.partial(whole_kernel, names, owners, unit), out_...  51.9 us

profile of v7, /device:TPU:1, one launch (start us, length us, event | category | flops | bytes accessed | tf_op | source)
XLA Modules:
  0.0 53.3 jit_solution(6052274231602738078)
XLA Ops:
  0.6 51.9 %shard_map.247 = (bf16[6,12,2,192]{3,2,1,0:T(2,128)(2,1)S(1)}, f32[160,192]{1,0:T(8,128)S(1)}, f32[64,192]{1,0:T(8,128)S(1)}) custom-call(bf16[5,6,24,48]{3,2,1,0:T(8,128)(2,1)} %refs_0_.1, bf16[4,24,48]{2,1,0:T(8,128)(2,1)} %refs_1_.1, bf16[4,144,48]{2,1,0:T(8,128)(2,1)} %constant.26.clone.refs_2_, f32[144,1]{1,0:T(8,128)} %constant.27.clone.refs_3_, ...), custom_call_target="tpu_custom_call" | custom-call | tf_op jit(solution)/shard_map/pallas_call | solution.py:580
  52.5 0.7 %shard_map.248 = (bf16[6,12,2,192]{3,2,1,0:T(2,128)(2,1)}, f32[160,192]{1,0:T(8,128)}, f32[64,192]{1,0:T(8,128)}) custom-call(bf16[6,12,2,192]{3,2,1,0:T(2,128)(2,1)S(1)} %get-tuple-element.9.refs_0_, f32[160,192]{1,0:T(8,128)S(1)} %get-tuple-element.10.refs_1_, f32[64,192]{1,0:T(8,128)S(1)} %get-tuple-element.11.refs_2_), custom_call_target="tpu_custom_call" | custom-call | tf_op jit(solution)/shard_map/pallas_call | solution.py:625

commit v8 on v7

--- a/solution.py
+++ b/solution.py
@@ -308,11 +308,17 @@
 class Loads:
     def __init__(self, names, sources, targets, sems):
         self.targets = dict(zip(names, targets))
-        self.copies = {}
-        for i, name in enumerate(names):
-            copy = pltpu.make_async_copy(sources[i], targets[i], sems.at[i])
-            copy.start()
-            self.copies[name] = copy
+        self.copies = {n: pltpu.make_async_copy(*refs) for n, refs in zip(names, self.pairs(sources, targets, sems))}
+        self.pending = list(names)
+
+    @staticmethod
+    def pairs(sources, targets, sems):
+        return [(source, targets[i], sems.at[i]) for i, source in enumerate(sources)]
+
+    def start(self, count):
+        for name in self.pending[:count]:
+            self.copies[name].start()
+        self.pending = self.pending[count:]
 
     def __getitem__(self, name):
         copy = self.copies.pop(name, None)
@@ -357,6 +363,7 @@
         result,
         sems,
     ) = refs[count : -count - 1]
+    consts.start(11)
     routes = Routes()
     lon, lat, section = routes.lon, routes.lat, routes.section
     lon_count, lat_count, section_count = routes.lons, routes.lats, routes.sections
@@ -364,11 +371,14 @@
     owner, mine = routes.near_index(), routes.far_index()
     barrier = pltpu.get_barrier_semaphore()
     corners = sorted(itertools.product(range(2), repeat=3), reverse=True)
-    targets = [routes.corner(d, sign) for d in corners[:-1] for sign in (-1, 1) if d != (0, 1, 0) or sign > 0]
+    targets = [routes.corner(d, sign) for d in corners if d[0] or sum(d) > 1 for sign in (-1, 1)]
     targets += [routes.far_peer(step) for step in routes.far_steps]
     targets += [routes.near_peer(step) for step in routes.near_steps]
     for target in targets:
         pl.semaphore_signal(barrier, inc=1, device_id=target, device_id_type=MESH)
+    consts.start(count)
+    for name in names[:11]:
+        consts[name]
 
     field[240:256, :] = jnp.zeros((16, 48), f32)
     field[496:512, :] = jnp.zeros((16, 48), f32)

time: 53.4 us -> 53.2 us (level)
  no operation moved by 1% of the time
where the time goes in v8:
time: 53.2 us; the launch traced here: 53.1 us
  Pallas kernels  52.4 us (98%)
  between operations  0.64 us (1%)
    pallas_call x1, Pallas kernels, on_device(): pl.pallas_call(functools.partial(whole_kernel, names, owners, unit), out_...  51.7 us

profile of v8, /device:TPU:1, one launch (start us, length us, event | category | flops | bytes accessed | tf_op | source)
XLA Modules:
  0.0 53.1 jit_solution(15637242939010905741)
XLA Ops:
  0.6 51.7 %shard_map.247 = (bf16[6,12,2,192]{3,2,1,0:T(2,128)(2,1)S(1)}, f32[160,192]{1,0:T(8,128)S(1)}, f32[64,192]{1,0:T(8,128)S(1)}) custom-call(bf16[5,6,24,48]{3,2,1,0:T(8,128)(2,1)} %refs_0_.1, bf16[4,24,48]{2,1,0:T(8,128)(2,1)} %refs_1_.1, bf16[4,144,48]{2,1,0:T(8,128)(2,1)} %constant.26.clone.refs_2_, f32[144,1]{1,0:T(8,128)} %constant.27.clone.refs_3_, ...), custom_call_target="tpu_custom_call" | custom-call | tf_op jit(solution)/shard_map/pallas_call | solution.py:590
  52.3 0.7 %shard_map.248 = (bf16[6,12,2,192]{3,2,1,0:T(2,128)(2,1)}, f32[160,192]{1,0:T(8,128)}, f32[64,192]{1,0:T(8,128)}) custom-call(bf16[6,12,2,192]{3,2,1,0:T(2,128)(2,1)S(1)} %get-tuple-element.9.refs_0_, f32[160,192]{1,0:T(8,128)S(1)} %get-tuple-element.10.refs_1_, f32[64,192]{1,0:T(8,128)S(1)} %get-tuple-element.11.refs_2_), custom_call_target="tpu_custom_call" | custom-call | tf_op jit(solution)/shard_map/pallas_call | solution.py:635
